TPU v7x, 32 devices: a whole 2x2x4 slice. The times are simulated.
32 devices in a mesh: dp: 2 (over x), ctx: 4 (over y, core), tensor: 4 (over z).
Axes of the slice: x: 2, y: 2, z: 4, core: 2. Of those that a mesh axis runs over, the one named last changes fastest.
Arguments:
- hidden: bfloat16 [2, 16384, 2560], P('dp', 'ctx', 'tensor'), may hold values from -6 to 6
- depth: int32 [2, 16384], P('dp', 'ctx'), may hold values from 1 to 4, as said below
- qkv_weight: bfloat16 [2560, 3, 2560], P(None, None, 'tensor'), may hold values from -0.125 to 0.125
- out_weight: bfloat16 [2560, 2560], P('tensor'), may hold values from -0.125 to 0.125
Outputs:
- update: bfloat16 [2, 16384, 2560], P('dp', 'ctx', 'tensor')
Inputs may be any that keep to these rules, and one draw needn't show every extreme that they name: In every aligned block of 4096 positions of a document at most 1024 tokens have depth at least 3, and some block has exactly 1024; over all documents exactly 4096 tokens do.
All inputs are finite; a program needn't handle non-finite values.
Results may differ from a plain program's by a relative error of at most 0.012.
The roundings to bfloat16 on the way count: a program that leaves them out, or rounds other values in their place, can miss the bound.
Values may be sent and summed in bfloat16 or wider, within the bound.
A program may use at most 256 MiB of HBM per device.

v0:
```python
import functools

import jax
import jax.numpy as jnp
from jax import lax
from jax.experimental import pallas as pl
from jax.experimental.pallas import tpu as pltpu
from jax.sharding import PartitionSpec as P

HD = 128
RECURSION = 3
CAP = 1024
ACT_DEV = 512

score_scale = 0.25
norm_epsilon = 1e-05
head_epsilon = 1e-06
VMEM_LIMIT = 60 * 1024 * 1024
PLANE = ("dp", "ctx")


def project_kernel(x_ref, w_ref, q_ref, kv_ref, normed):
    part = pl.program_id(0)
    shards, rows, width = x_ref.shape

    @pl.when(part == 0)
    def _():
        total = jnp.zeros((rows, 1), jnp.float32)
        for z in range(shards):
            wide = x_ref[z].astype(jnp.float32)
            total = total + jnp.sum(wide * wide, axis=1, keepdims=True)
        factor = lax.rsqrt(total / (shards * width) + norm_epsilon)
        for z in range(shards):
            normed[z] = (x_ref[z].astype(jnp.float32) * factor).astype(jnp.bfloat16)

    acc = jnp.dot(normed[0], w_ref[0, :width], preferred_element_type=jnp.float32)
    for z in range(1, shards):
        acc = acc + jnp.dot(normed[z], w_ref[0, z * width : (z + 1) * width], preferred_element_type=jnp.float32)
    heads = acc.shape[1] // HD

    def head_normed(scale):
        parts = []
        for h in range(heads):
            head = acc[:, h * HD : (h + 1) * HD]
            factor = lax.rsqrt(jnp.mean(head * head, axis=1, keepdims=True) + head_epsilon) * scale
            parts.append((head * factor).astype(jnp.bfloat16))
        return parts

    @pl.when(part == 0)
    def _():
        for h, value in enumerate(head_normed(score_scale)):
            q_ref[:, h * HD : (h + 1) * HD] = value

    @pl.when(part == 1)
    def _():
        for h, value in enumerate(head_normed(1.0)):
            kv_ref[0, :, h * HD : (h + 1) * HD] = value

    @pl.when(part == 2)
    def _():
        kv_ref[0] = acc.astype(jnp.bfloat16)


def project(rows_all, weight):
    shards, rows, width = rows_all.shape
    head_width = weight.shape[2]
    flops = 2 * rows * shards * width * 3 * head_width
    return pl.pallas_call(
        project_kernel,
        grid=(3,),
        out_shape=[
            jax.ShapeDtypeStruct((rows, head_width), jnp.bfloat16),
            jax.ShapeDtypeStruct((2, rows, head_width), jnp.bfloat16),
        ],
        in_specs=[
            pl.BlockSpec((shards, rows, width), lambda p: (0, 0, 0)),
            pl.BlockSpec((1, shards * width, head_width), lambda p: (p, 0, 0)),
        ],
        out_specs=[
            pl.BlockSpec((rows, head_width), lambda p: (0, 0)),
            pl.BlockSpec((1, rows, head_width), lambda p: (jnp.maximum(p - 1, 0), 0, 0)),
        ],
        scratch_shapes=[pltpu.VMEM((shards, rows, width), jnp.bfloat16)],
        compiler_params=pltpu.CompilerParams(vmem_limit_bytes=VMEM_LIMIT),
        cost_estimate=pl.CostEstimate(flops=flops, bytes_accessed=2 * weight.size, transcendentals=0),
        name="project",
    )(rows_all, weight)


def gather_kernel(pieces, kv_ref, out_ref, send_sem, recv_sem, local_sem):
    x, place = lax.axis_index("dp"), lax.axis_index("ctx")
    y, core = place // 2, lax.rem(place, 2)
    rows = kv_ref.shape[1] // pieces

    def block(flip_x, flip_y, flip_core):
        return (x ^ flip_x) * 4 + (y ^ flip_y) * 2 + (core ^ flip_core)

    def device(flip_x, flip_y, flip_core):
        return {"dp": x ^ flip_x, "ctx": (y ^ flip_y) * 2 + (core ^ flip_core)}

    sibling, across_x, across_y = device(0, 0, 1), device(1, 0, 0), device(0, 1, 0)
    barrier = pltpu.get_barrier_semaphore()
    for target in (sibling, across_x, across_y):
        pl.semaphore_signal(barrier, inc=1, device_id=target, device_id_type=pl.DeviceIdType.MESH)
    pl.semaphore_wait(barrier, 3)

    me = block(0, 0, 0)
    local = pltpu.make_async_copy(kv_ref, out_ref.at[me], local_sem)
    local.start()
    sends = []

    def send(origin, route, piece, target, own=False):
        window = pl.ds(piece * rows, rows)
        copy = pltpu.make_async_remote_copy(
            src_ref=kv_ref.at[:, window] if own else out_ref.at[origin, :, window],
            dst_ref=out_ref.at[origin, :, window],
            send_sem=send_sem.at[route, piece],
            recv_sem=recv_sem.at[route, piece],
            device_id=target,
            device_id_type=pl.DeviceIdType.MESH,
        )
        copy.start()
        sends.append(copy)

    def arrive(origin, route, piece):
        window = pl.ds(piece * rows, rows)
        pltpu.make_async_remote_copy(
            src_ref=out_ref.at[origin, :, window],
            dst_ref=out_ref.at[origin, :, window],
            send_sem=send_sem.at[route, piece],
            recv_sem=recv_sem.at[route, piece],
            device_id=sibling,
            device_id_type=pl.DeviceIdType.MESH,
        ).wait_recv()

    for piece in range(pieces):
        send(me, 1, piece, across_x, True)
        send(me, 2, piece, across_y, True)
        send(me, 0, piece, sibling, True)
    first = core == 0
    onward = jnp.where(first, block(0, 1, 0), block(1, 0, 0))
    onward_device = {
        "dp": jnp.where(first, x ^ 1, x),
        "ctx": jnp.where(first, place, (y ^ 1) * 2 + core),
    }
    for piece in range(pieces):
        arrive(block(1, 0, 0), 1, piece)
        arrive(block(0, 1, 0), 2, piece)
        send(onward, 3, piece, onward_device)
        send(block(1, 0, 0), 4, piece, sibling)
        send(block(0, 1, 0), 5, piece, sibling)
    for piece in range(pieces):
        arrive(block(1, 1, 0), 3, piece)
        send(block(1, 1, 0), 6, piece, sibling)
    for piece in range(pieces):
        arrive(block(0, 0, 1), 0, piece)
        arrive(block(1, 0, 1), 4, piece)
        arrive(block(0, 1, 1), 5, piece)
        arrive(block(1, 1, 1), 6, piece)
    for copy in sends:
        copy.wait_send()
    local.wait()


def gather_plane(kv, call):
    docs, ctx_count = lax.axis_size("dp"), lax.axis_size("ctx")
    if (docs, ctx_count) != (2, 4):
        return lax.all_gather(kv, PLANE, axis=0)
    pieces = 8
    plane = docs * ctx_count
    return pl.pallas_call(
        functools.partial(gather_kernel, pieces),
        out_shape=jax.ShapeDtypeStruct((plane,) + kv.shape, kv.dtype),
        in_specs=[pl.BlockSpec(memory_space=pltpu.VMEM)],
        out_specs=pl.BlockSpec(memory_space=pl.ANY),
        scratch_shapes=[
            pltpu.SemaphoreType.DMA((7, pieces)),
            pltpu.SemaphoreType.DMA((7, pieces)),
            pltpu.SemaphoreType.DMA,
        ],
        compiler_params=pltpu.CompilerParams(collective_id=call, has_side_effects=True),
        cost_estimate=pl.CostEstimate(flops=0, bytes_accessed=60_000_000, transcendentals=0),
        name="gather_plane",
    )(kv)


def attend_kernel(docs, base, meta_ref, q_ref, *refs):
    w_ref, o_ref, total = refs[-3:]
    pairs = [(refs[i], refs[i + 1]) for i in range(0, len(refs) - 3, 2)]
    head = pl.program_id(0)
    plane, stripes, size, _ = refs[0].shape
    period = plane * size
    rows = stripes * size
    me = meta_ref[docs]
    row = lax.broadcasted_iota(jnp.int32, (rows, 1), 0)
    q_index = (base + row // size) * period + me * size + lax.rem(row, size)
    begin = jnp.zeros((rows, 1), jnp.int32)
    for d in range(docs):
        begin = jnp.where(q_index >= meta_ref[d], meta_ref[d], begin)
    lane = lax.broadcasted_iota(jnp.int32, (1, period), 1)
    query = q_ref[...]
    num = jnp.zeros((rows, HD), jnp.float32)
    den = jnp.zeros((rows, 1), jnp.float32)
    at = 0
    for k_ref, v_ref in pairs:
        for k in range(stripes):
            keys = k_ref[:, k].reshape(period, HD)
            values = v_ref[:, k].reshape(period, HD)
            scores = lax.dot_general(query, keys, (((1,), (1,)), ((), ())), preferred_element_type=jnp.float32)
            allowed = lane >= begin - at * period
            if at >= base:
                allowed = allowed & (lane <= q_index - at * period)
            weights = jnp.where(allowed, jnp.exp(scores), 0.0)
            den = den + jnp.sum(weights, axis=1, keepdims=True)
            num = num + jnp.dot(weights.astype(jnp.bfloat16), values, preferred_element_type=jnp.float32)
            at += 1
    context = (num / den).astype(jnp.bfloat16)
    term = jnp.dot(context, w_ref[...], preferred_element_type=jnp.float32)

    @pl.when(head == 0)
    def _():
        total[...] = term

    @pl.when(head > 0)
    def _():
        total[...] += term

    @pl.when(head == pl.num_programs(0) - 1)
    def _():
        width = o_ref.shape[2]
        for z in range(o_ref.shape[0]):
            o_ref[z] = total[:, z * width : (z + 1) * width].astype(jnp.bfloat16)


def attend(meta, queries, kvs, out_weight, shards, docs, stripes):
    rows, head_width = queries.shape
    plane = kvs[0].shape[0]
    size = rows // stripes
    heads = head_width // HD
    operands, specs = [], []
    for kv in kvs:
        kv = kv.reshape(plane, 2, stripes, size, head_width)
        for which in range(2):
            operands.append(kv)
            specs.append(
                pl.BlockSpec((plane, None, stripes, size, HD), lambda h, m, which=which: (0, which, 0, 0, h))
            )
    width = out_weight.shape[1]
    operands.append(out_weight)
    specs.append(pl.BlockSpec((HD, width), lambda h, m: (h, 0)))
    pairs = rows * plane * rows * len(kvs)
    return pl.pallas_call(
        functools.partial(attend_kernel, docs, (len(kvs) - 1) * stripes),
        grid_spec=pltpu.PrefetchScalarGridSpec(
            num_scalar_prefetch=1,
            grid=(heads,),
            in_specs=[pl.BlockSpec((rows, HD), lambda h, m: (0, h))] + specs,
            out_specs=pl.BlockSpec((shards, rows, width // shards), lambda h, m: (0, 0, 0)),
            scratch_shapes=[pltpu.VMEM((rows, width), jnp.float32)],
        ),
        out_shape=jax.ShapeDtypeStruct((shards, rows, width // shards), jnp.bfloat16),
        compiler_params=pltpu.CompilerParams(vmem_limit_bytes=VMEM_LIMIT),
        cost_estimate=pl.CostEstimate(
            flops=4 * pairs * head_width, bytes_accessed=4 * kvs[0].size, transcendentals=pairs * heads
        ),
        name="attend",
    )(meta, queries, *operands)


def per_device(hidden, depth, qkv_weight, out_weight):
    tokens = hidden[0]
    local_len = tokens.shape[0]
    docs = lax.axis_size("dp")
    ctx_count = lax.axis_size("ctx")
    shards = lax.axis_size("tensor")
    plane = docs * ctx_count
    me = lax.axis_index("dp") * ctx_count + lax.axis_index("ctx")
    size = CAP // plane
    stripes = ACT_DEV // size

    active = depth[0] >= RECURSION
    ones = active.astype(jnp.int32)
    counts = lax.all_gather(jnp.sum(ones)[None], PLANE, axis=0, tiled=True)
    ends = jnp.cumsum(counts)
    starts = ends - counts
    rank = jnp.cumsum(ones) - 1
    slot = jnp.where(active, lax.rem(starts[me] + rank, CAP), -1)
    onehot = (jnp.arange(CAP, dtype=jnp.int32)[:, None] == slot[None, :]).astype(jnp.bfloat16)
    dealt = jnp.dot(onehot, tokens, preferred_element_type=jnp.float32).astype(jnp.bfloat16)
    received = lax.all_to_all(dealt.reshape(plane, size, -1), PLANE, 0, 0)

    index = (
        jnp.arange(stripes, dtype=jnp.int32)[:, None] * CAP
        + me * size
        + jnp.arange(size, dtype=jnp.int32)[None, :]
    )
    owned = (index[None] >= starts[:, None, None]) & (index[None] < ends[:, None, None])
    zero = jnp.zeros((), jnp.bfloat16)
    packed = jnp.where(owned[0][:, :, None], received[0][None], zero)
    for b in range(1, plane):
        packed = jnp.where(owned[b][:, :, None], received[b][None], packed)
    packed = packed.reshape(ACT_DEV, -1)

    chunks = 2
    chunk_stripes = stripes // chunks
    chunk_rows = ACT_DEV // chunks
    weight = jnp.transpose(qkv_weight, (1, 0, 2))
    meta = jnp.concatenate([starts[::ctx_count], me[None]]).astype(jnp.int32)
    rows_all = [
        lax.all_gather(packed[c * chunk_rows : (c + 1) * chunk_rows], "tensor", axis=0) for c in range(chunks)
    ]
    kvs, backs = [], []
    for c in range(chunks):
        queries, kv = project(rows_all[c], weight)
        kvs.append(gather_plane(kv, c))
        terms = attend(meta, queries, kvs, out_weight, shards, docs, chunk_stripes)
        backs.append(lax.psum_scatter(terms, "tensor", scatter_dimension=0))
    rows_back = jnp.concatenate(backs, axis=0)

    rows_back = rows_back.reshape(stripes, size, -1)
    returned = jnp.where(owned[:, 0][:, :, None], rows_back[0][None], zero)
    for k in range(1, stripes):
        returned = jnp.where(owned[:, k][:, :, None], rows_back[k][None], returned)
    landed = lax.all_to_all(returned, PLANE, 0, 0).reshape(CAP, -1)
    spread = (slot[:, None] == jnp.arange(CAP, dtype=jnp.int32)[None, :]).astype(jnp.bfloat16)
    update = jnp.dot(spread, landed, preferred_element_type=jnp.float32).astype(jnp.bfloat16)
    return update[None]


def solution(mesh):
    placed = (P("dp", "ctx", "tensor"), P("dp", "ctx"), P(None, None, "tensor"), P("tensor", None))
    return jax.shard_map(
        per_device, mesh=mesh, in_specs=placed, out_specs=P("dp", "ctx", "tensor"), check_vma=False
    )
```

profile of v0, /device:TPU:0, one launch (start us, length us, event | category | flops | bytes accessed | tf_op | source)
XLA Modules:
  0.0 261.3 jit_solution(12537284861384939891)
XLA Ops:
  6.5 0.8 fusion.14
  7.3 0.6 convert_reduce_fusion
  8.0 1.3 dynamic-slice
  9.2 1.4 dynamic-update-slice
  10.6 9.5 %all-reduce = s32[8]{0:T(128)S(1)} all-reduce(s32[8]{0:T(128)S(1)} %dynamic-update-slice), channel_id=1, replica_groups=mesh['dp'=2,'ctx'=4,'tensor'=4] {'dp','ctx'}, use_global_device_ids=true, to_apply=%add | all-reduce | flops 8 | bytes 64
  20.1 0.3 reduce-window.20
  20.4 0.2 reduce-window.19
  20.6 0.1 slice.143
  20.6 0.1 reduce-window.21
  20.7 0.1 slice_reduce_fusion
  20.8 0.6 dynamic_slice.3
  21.4 0.7 fusion.11
  22.1 0.8 fusion.13
  22.9 10.8 %fusion.7 = bf16[1024,640]{1,0:T(8,128)(2,1)} fusion(bf16[1,4096,640]{2,1,0:T(8,128)(2,1)} %param.4, s32[4096]{0:T(1024)S(1)} %bitcast.88), kind=kOutput, calls=%fused_computation.9 | convolution fusion | flops 5373558784 | bytes 6569984 | tf_op jit(solution)/shard_map/dot_general | solution.py:289
  33.7 3.6 %all-to-all-start = ((bf16[8,128,640]{2,1,0:T(8,128)(2,1)}), bf16[8,128,640]{2,1,0:T(8,128)(2,1)S(1)}, u32[]{:S(2)}, u32[]{:S(2)}) async-start(bf16[8,128,640]{2,1,0:T(8,128)(2,1)} %bitcast.12), calls=%async_computation | async-start | bytes 2621440 | tf_op jit(solution)/shard_map/all_to_all | solution.py:290
  37.3 0.0 all-gather.5.cloned.1.call-start
  37.3 0.1 iota_add_fusion
  37.4 0.1 compare_and_fusion
  37.6 16.9 %all-to-all-done = bf16[8,128,640]{2,1,0:T(8,128)(2,1)S(1)} async-done(((bf16[8,128,640]{2,1,0:T(8,128)(2,1)}), bf16[8,128,640]{2,1,0:T(8,128)(2,1)S(1)}, u32[]{:S(2)}, u32[]{:S(2)}) %all-to-all-start) | async-done | bytes 1310752 | tf_op jit(solution)/shard_map/all_to_all | solution.py:290
  54.5 0.1 slice_bitcast_fusion.11
  54.6 1.0 select_select_fusion.1
  55.6 0.9 fusion.16
  56.5 0.0 all-gather.5.cloned.1.call-update
  56.5 0.0 all-gather.3.cloned.1.call-start
  56.5 0.7 all-gather.3.cloned.1.call-update
  57.2 0.2 reduce-scatter.5.cloned.1.call-start
  57.5 0.1 slice.113
  57.5 0.6 pad_add_fusion.meta_ref
  58.1 31.3 %all-gather.5.cloned.1.call-done.x_ref = bf16[4,256,640]{2,1,0:T(8,128)(2,1)} async-done(((bf16[1,256,640]{2,1,0:T(8,128)(2,1)}), bf16[4,256,640]{2,1,0:T(8,128)(2,1)}) %all-gather.5.cloned.1.call-update) | async-done | bytes 1310736 | tf_op jit(solution)/shard_map/all_gather | solution.py:310
  89.4 8.5 %project.3 = (bf16[256,640]{1,0:T(8,128)(2,1)}, bf16[2,256,640]{2,1,0:T(8,128)(2,1)}) custom-call(bf16[4,256,640]{2,1,0:T(8,128)(2,1)} %all-gather.5.cloned.1.call-done.x_ref, bf16[3,2560,640]{2,1,0:T(8,128)(2,1)} %bitcast.81), custom_call_target="tpu_custom_call" | custom-call | flops 2516582400 | bytes 9830400 | tf_op jit(solution)/shard_map/project/pallas_call | solution.py:68
  97.9 27.4 %gather_plane.2 = bf16[8,2,256,640]{3,2,1,0:T(8,128)(2,1)} custom-call(bf16[2,256,640]{2,1,0:T(8,128)(2,1)} %get-tuple-element.10.kv_ref), custom_call_target="tpu_custom_call" | custom-call | bytes 60000000 | tf_op jit(solution)/shard_map/gather_plane/pallas_call | solution.py:171
  125.4 13.1 %attend.3 = bf16[4,256,640]{2,1,0:T(8,128)(2,1)} custom-call(s32[3]{0:T(128)} %pad_add_fusion.meta_ref, bf16[256,640]{1,0:T(8,128)(2,1)} %get-tuple-element.12.q_ref, bf16[8,2,2,128,640]{4,3,2,1,0:T(8,128)(2,1)} %bitcast.75, bf16[8,2,2,128,640]{4,3,2,1,0:T(8,128)(2,1)} %bitcast.76, bf16[640,2560]{1,0:T(8,128)(2,1)} %refs_2_.1), custom_call_target="tpu_custom_call" | custom-call | flops 1342177280 | bytes 10485760 | tf_op jit(solution)/shard_map/attend/pallas_call | solution.py:252
  138.5 0.0 reduce-scatter.5.cloned.1.call-update
  138.5 0.0 reduce-scatter.3.cloned.1.call-start
  138.6 0.0 all-gather.3.cloned.1.call-done.x_ref
  138.6 8.7 %project.2 = (bf16[256,640]{1,0:T(8,128)(2,1)}, bf16[2,256,640]{2,1,0:T(8,128)(2,1)}) custom-call(bf16[4,256,640]{2,1,0:T(8,128)(2,1)} %all-gather.3.cloned.1.call-done.x_ref, bf16[3,2560,640]{2,1,0:T(8,128)(2,1)} %bitcast.82), custom_call_target="tpu_custom_call" | custom-call | flops 2516582400 | bytes 9830400 | tf_op jit(solution)/shard_map/project/pallas_call | solution.py:68
  147.3 27.7 %gather_plane.3 = bf16[8,2,256,640]{3,2,1,0:T(8,128)(2,1)} custom-call(bf16[2,256,640]{2,1,0:T(8,128)(2,1)} %get-tuple-element.11.kv_ref), custom_call_target="tpu_custom_call" | custom-call | bytes 60000000 | tf_op jit(solution)/shard_map/gather_plane/pallas_call | solution.py:171
  175.0 17.2 %attend.2 = bf16[4,256,640]{2,1,0:T(8,128)(2,1)} custom-call(s32[3]{0:T(128)} %pad_add_fusion.meta_ref, bf16[256,640]{1,0:T(8,128)(2,1)} %get-tuple-element.9.q_ref, bf16[8,2,2,128,640]{4,3,2,1,0:T(8,128)(2,1)} %bitcast.77, bf16[8,2,2,128,640]{4,3,2,1,0:T(8,128)(2,1)} %bitcast.78, bf16[8,2,2,128,640]{4,3,2,1,0:T(8,128)(2,1)} %bitcast.79, ...), custom_call_target="tpu_custom_call" | custom-call | flops 2684354560 | bytes 10485760 | tf_op jit(solution)/shard_map/attend/pallas_call | solution.py:252
  192.2 0.0 reduce-scatter.3.cloned.1.call-update
  192.3 0.0 reduce-scatter.5.cloned.1.call-done
  192.3 1.0 slice_bitcast_fusion.1
  193.3 29.1 %reduce-scatter.3.cloned.1.call-done = bf16[1,256,640]{2,1,0:T(8,128)(2,1)} async-done(((bf16[4,256,640]{2,1,0:T(8,128)(2,1)}), bf16[1,256,640]{2,1,0:T(8,128)(2,1)}) %reduce-scatter.3.cloned.1.call-update) | async-done | bytes 327696 | tf_op jit(solution)/shard_map/reduce_scatter | solution.py:317
  222.5 1.0 slice_bitcast_fusion.3
  223.5 1.0 select_select_fusion
  224.5 20.9 %all_to_all.10 = bf16[8,128,640]{2,1,0:T(8,128)(2,1)S(1)} all-to-all(bf16[8,128,640]{2,1,0:T(8,128)(2,1)S(1)} %select_select_fusion), channel_id=1, replica_groups=mesh['dp'=2,'ctx'=4,'tensor'=4] {'dp','ctx'}, dimensions={0} | all-to-all | bytes 2621440 | tf_op jit(solution)/shard_map/all_to_all | solution.py:324
  245.4 9.4 %fusion.5 = bf16[1,4096,640]{2,1,0:T(8,128)(2,1)} fusion(bf16[1024,640]{1,0:T(8,128)(2,1)S(1)} %bitcast.85, s32[4096]{0:T(1024)S(1)} %get-tuple-element.13), kind=kOutput, calls=%fused_computation.7 | convolution fusion | flops 5375524864 | bytes 6569984 | tf_op jit(solution)/shard_map/dot_general | solution.py:326
  (9 shorter events, 0.1 us)
Async XLA Ops:
  33.7 20.8 %all-to-all-start = ((bf16[8,128,640]{2,1,0:T(8,128)(2,1)}), bf16[8,128,640]{2,1,0:T(8,128)(2,1)S(1)}, u32[]{:S(2)}, u32[]{:S(2)}) async-start(bf16[8,128,640]{2,1,0:T(8,128)(2,1)} %bitcast.12), calls=%async_computation | async-start | bytes 2621440 | tf_op jit(solution)/shard_map/all_to_all | solution.py:290
  37.3 52.2 %all-gather.5.cloned.1.call-start = ((), (), s32[]{:S(2)}) async-start(), calls=%async_computation.5 | async-start | bytes 1638400 | tf_op jit(solution)/shard_map/all_gather | solution.py:310
  56.5 82.1 %all-gather.3.cloned.1.call-start = ((), (), s32[]{:S(2)}) async-start(), calls=%async_computation.4 | async-start | bytes 1638400 | tf_op jit(solution)/shard_map/all_gather | solution.py:310
  57.2 135.1 %reduce-scatter.5.cloned.1.call-start = ((), (), s32[]{:S(2)}) async-start(), calls=%async_computation.7 | async-start | bytes 1638400 | tf_op jit(solution)/shard_map/reduce_scatter | solution.py:317
  138.5 83.9 %reduce-scatter.3.cloned.1.call-start = ((), (), s32[]{:S(2)}) async-start(), calls=%async_computation.6 | async-start | bytes 1638400 | tf_op jit(solution)/shard_map/reduce_scatter | solution.py:317
Sparse Core Ops, SparseCore 0:
  56.6 32.7 all-gather.4
  91.0 31.6 all-gather.2
  138.7 30.1 reduce-scatter.4
  192.4 30.0 reduce-scatter.2
where the time goes:
time: 262 us; the launch traced here: 261 us
  Pallas kernels  103 us (39%)
  waiting for transfers between devices  78.1 us (30%)
  blocking collectives  30.4 us (12%)
  matrix products  20.2 us (8%)
  between operations  13.3 us (5%)
  local copies, waits for them, and re-layouts  6.63 us (3%)
  other arithmetic  6.09 us (2%)
  starting transfers between devices  3.91 us (1%)
    pallas_call x2, Pallas kernels, gather_plane(): pl.pallas_call(functools.partial(gather_kernel, pieces), out_shape=jax.Sh...  55.1 us
    all_gather x2, waiting for transfers between devices, per_device(): lax.all_gather(packed[c * chunk_rows:(c + 1) * chunk_rows], 'tensor', axi...  31.3 us
    pallas_call x2, Pallas kernels, attend(): pl.pallas_call(functools.partial(attend_kernel, docs, (len(kvs) - 1) * st...  30.4 us
    reduce_scatter x2, waiting for transfers between devices, per_device(): backs.append(lax.psum_scatter(terms, 'tensor', scatter_dimension=0))  29.2 us
    all_to_all x1, blocking collectives, per_device(): landed = lax.all_to_all(returned, PLANE, 0, 0).reshape(CAP, -1)  20.9 us
    pallas_call x2, Pallas kernels, project(): pl.pallas_call(project_kernel, grid=(3,), out_shape=[jax.ShapeDtypeStruct...  17.2 us
    all_to_all x1, waiting for transfers between devices, per_device(): received = lax.all_to_all(dealt.reshape(plane, size, -1), PLANE, 0, 0)  16.9 us
    dot_general x1, matrix products, per_device(): jnp.dot(onehot, tokens, preferred_element_type=jnp.float32)  10.8 us
  transfers between devices with their start and end apart: 5, of which 3 were waited for; matrix products, arithmetic and copies ran while one was open for 1% of the time, Pallas kernels for 39%

commit v1 on v0

--- a/solution.py
+++ b/solution.py
@@ -267,6 +267,381 @@
     )(meta, queries, *operands)
 
 
+def line_copy(src, dst, send_sem, recv_sem, to):
+    return pltpu.make_async_remote_copy(
+        src_ref=src,
+        dst_ref=dst,
+        send_sem=send_sem,
+        recv_sem=recv_sem,
+        device_id=to,
+        device_id_type=pl.DeviceIdType.MESH,
+    )
+
+
+def block_kernel(
+    docs, meta_ref, x_ref, w_hbm, wo_hbm, o_ref,
+    w, wo, xg, normed, query, kv, num, den, context, terms, from_right, from_left, final,
+    w_sem, a_send, a_recv, g_send, g_recv, r_send, r_recv,
+):
+    shards, rows, width = xg.shape
+    stripes, plane, _, size, head_width = kv.shape
+    heads = head_width // HD
+    period = plane * size
+    last = shards - 1
+    x, place, z = lax.axis_index("dp"), lax.axis_index("ctx"), lax.axis_index("tensor")
+    y, core = place // 2, lax.rem(place, 2)
+
+    def block(flip_x, flip_y, flip_core):
+        return (x ^ flip_x) * 4 + (y ^ flip_y) * 2 + (core ^ flip_core)
+
+    def device(flip_x, flip_y, flip_core):
+        return {"dp": x ^ flip_x, "ctx": (y ^ flip_y) * 2 + (core ^ flip_core)}
+
+    me = block(0, 0, 0)
+    sibling, across_x, across_y = device(0, 0, 1), device(1, 0, 0), device(0, 1, 0)
+    left, right = {"tensor": z - 1}, {"tensor": z + 1}
+
+    loads = [pltpu.make_async_copy(w_hbm.at[p], w.at[p], w_sem.at[p]) for p in range(3)]
+    loads.append(pltpu.make_async_copy(wo_hbm, wo, w_sem.at[3]))
+    for which in (1, 2, 0, 3):
+        loads[which].start()
+
+    barrier = pltpu.get_barrier_semaphore()
+    for target in (sibling, across_x, across_y):
+        pl.semaphore_signal(barrier, inc=1, device_id=target, device_id_type=pl.DeviceIdType.MESH)
+
+    @pl.when(z > 0)
+    def _():
+        pl.semaphore_signal(barrier, inc=1, device_id=left, device_id_type=pl.DeviceIdType.MESH)
+
+    @pl.when(z < last)
+    def _():
+        pl.semaphore_signal(barrier, inc=1, device_id=right, device_id_type=pl.DeviceIdType.MESH)
+
+    pl.semaphore_wait(barrier, 3 + jnp.where(z > 0, 1, 0) + jnp.where(z < last, 1, 0))
+
+    def rows_of(s):
+        return pl.ds(s * size, size)
+
+    def feature_copy(s, way, hop):
+        origin = z + hop if way == 0 else z - hop
+        piece = xg.at[origin, rows_of(s)]
+        source = x_ref.at[rows_of(s)] if hop == 0 else piece
+        return line_copy(source, piece, a_send.at[way, s, hop], a_recv.at[way, s, hop], left if way == 0 else right)
+
+    def feature_sent(way, hop):
+        return (z > 0) & (z + hop <= last) if way == 0 else (z < last) & (z - hop >= 0)
+
+    def feature_first(s):
+        for way in range(2):
+
+            @pl.when(feature_sent(way, 0))
+            def _():
+                feature_copy(s, way, 0).start()
+
+    def feature_hop(s, hop):
+        for way in range(2):
+
+            @pl.when((z + hop <= last) if way == 0 else (z - hop >= 0))
+            def _():
+                origin = z + hop if way == 0 else z - hop
+                piece = xg.at[origin, rows_of(s)]
+                line_copy(
+                    piece, piece, a_send.at[way, s, hop - 1], a_recv.at[way, s, hop - 1], left if way == 0 else right
+                ).wait_recv()
+
+            if hop < last:
+
+                @pl.when(feature_sent(way, hop))
+                def _():
+                    feature_copy(s, way, hop).start()
+
+    def feature_end():
+        for s in range(stripes):
+            for way in range(2):
+                for hop in range(last):
+
+                    @pl.when(feature_sent(way, hop))
+                    def _():
+                        feature_copy(s, way, hop).wait_send()
+
+    first = core == 0
+    onward = jnp.where(first, block(0, 1, 0), block(1, 0, 0))
+    onward_device = {
+        "dp": jnp.where(first, x ^ 1, x),
+        "ctx": jnp.where(first, place, (y ^ 1) * 2 + core),
+    }
+    sent = []
+
+    def kv_send(s, origin, route, target):
+        copy = line_copy(kv.at[s, origin], kv.at[s, origin], g_send.at[s, route], g_recv.at[s, route], target)
+        copy.start()
+        sent.append(copy)
+
+    def kv_arrive(s, origin, route):
+        line_copy(
+            kv.at[s, origin], kv.at[s, origin], g_send.at[s, route], g_recv.at[s, route], sibling
+        ).wait_recv()
+
+    def kv_own(s):
+        kv_send(s, me, 1, across_x)
+        kv_send(s, me, 2, across_y)
+        kv_send(s, me, 0, sibling)
+
+    def kv_near(s):
+        kv_arrive(s, block(1, 0, 0), 1)
+        kv_arrive(s, block(0, 1, 0), 2)
+        kv_send(s, onward, 3, onward_device)
+        kv_send(s, block(1, 0, 0), 4, sibling)
+        kv_send(s, block(0, 1, 0), 5, sibling)
+
+    def kv_far(s):
+        kv_arrive(s, block(1, 1, 0), 3)
+        kv_send(s, block(1, 1, 0), 6, sibling)
+
+    def kv_all(s):
+        kv_arrive(s, block(0, 0, 1), 0)
+        kv_arrive(s, block(1, 0, 1), 4)
+        kv_arrive(s, block(0, 1, 1), 5)
+        kv_arrive(s, block(1, 1, 1), 6)
+
+    def normalize(s):
+        total = jnp.zeros((size, 1), jnp.float32)
+        for j in range(shards):
+            wide = xg[j, rows_of(s)].astype(jnp.float32)
+            total = total + jnp.sum(wide * wide, axis=1, keepdims=True)
+        factor = lax.rsqrt(total / (shards * width) + norm_epsilon)
+        for j in range(shards):
+            normed[:, j * width : (j + 1) * width] = (xg[j, rows_of(s)].astype(jnp.float32) * factor).astype(
+                jnp.bfloat16
+            )
+
+    def head_normed(acc, scale):
+        parts = []
+        for h in range(heads):
+            head = acc[:, h * HD : (h + 1) * HD]
+            factor = lax.rsqrt(jnp.mean(head * head, axis=1, keepdims=True) + head_epsilon) * scale
+            parts.append((head * factor).astype(jnp.bfloat16))
+        return parts
+
+    def part_of(which):
+        return jnp.dot(normed[...], w[which], preferred_element_type=jnp.float32)
+
+    def project_kv(s):
+        normalize(s)
+        if s == 0:
+            loads[1].wait()
+        for h, value in enumerate(head_normed(part_of(1), 1.0)):
+            kv[s, me, 0, :, h * HD : (h + 1) * HD] = value
+        if s == 0:
+            loads[2].wait()
+        kv[s, me, 1] = part_of(2).astype(jnp.bfloat16)
+
+    def project_q(s):
+        if s == 0:
+            loads[0].wait()
+        for h, value in enumerate(head_normed(part_of(0), score_scale)):
+            query[rows_of(s), h * HD : (h + 1) * HD] = value
+
+    row = lax.broadcasted_iota(jnp.int32, (size, 1), 0)
+    lane = lax.broadcasted_iota(jnp.int32, (1, period), 1)
+
+    def begin_of(s):
+        q_index = s * period + me * size + row
+        begin = jnp.zeros((size, 1), jnp.int32)
+        for d in range(docs):
+            begin = jnp.where(q_index >= meta_ref[d], meta_ref[d], begin)
+        return begin
+
+    def attend(s, steps):
+        begin = begin_of(s)
+
+        def one_head(h, carry):
+            at = pl.ds(pl.multiple_of(h * HD, HD), HD)
+            lines = query[rows_of(s), at]
+            top = jnp.zeros((size, HD), jnp.float32) if steps[0] == 0 else num[s, :, at]
+            low = jnp.zeros((size, 1), jnp.float32) if steps[0] == 0 else den[s, :, at][:, :1]
+            for t in steps:
+                keys = kv[t, :, 0, :, at].reshape(period, HD)
+                values = kv[t, :, 1, :, at].reshape(period, HD)
+                scores = lax.dot_general(lines, keys, (((1,), (1,)), ((), ())), preferred_element_type=jnp.float32)
+                allowed = lane >= begin - t * period
+                if t == s:
+                    allowed = allowed & (lane <= me * size + row)
+                weights = jnp.where(allowed, jnp.exp(scores), 0.0)
+                low = low + jnp.sum(weights, axis=1, keepdims=True)
+                top = top + jnp.dot(weights.astype(jnp.bfloat16), values, preferred_element_type=jnp.float32)
+            if steps[-1] == s:
+                context[:, at] = (top / low).astype(jnp.bfloat16)
+            else:
+                num[s, :, at] = top
+                den[s, :, at] = jnp.broadcast_to(low, (size, HD))
+            return carry
+
+        lax.fori_loop(0, heads, one_head, 0)
+
+    def early(s):
+        if s > 0:
+            attend(s, list(range(s)))
+
+    def late(s):
+        attend(s, [s])
+
+    def project_out(s):
+        if s == 0:
+            loads[3].wait()
+        for j in range(shards):
+            terms[s, j] = jnp.dot(
+                context[...], wo[:, j * width : (j + 1) * width], preferred_element_type=jnp.float32
+            ).astype(jnp.bfloat16)
+
+    def sum_copy(s, way, d):
+        land = from_right if way == 0 else from_left
+        return line_copy(
+            terms.at[s, d], land.at[s, d], r_send.at[way, s, d], r_recv.at[way, s, d], left if way == 0 else right
+        )
+
+    def sum_sent(way, d):
+        return (z > d) if way == 0 else (z < d)
+
+    def sum_step(s, way, d):
+        inner = (z < last) if way == 0 else (z > 0)
+        land = from_right if way == 0 else from_left
+
+        @pl.when(sum_sent(way, d) & inner)
+        def _():
+            sum_copy(s, way, d).wait_recv()
+            terms[s, d] = (terms[s, d].astype(jnp.float32) + land[s, d].astype(jnp.float32)).astype(jnp.bfloat16)
+
+        @pl.when(sum_sent(way, d))
+        def _():
+            sum_copy(s, way, d).start()
+
+    def order(way, k):
+        return k if way == 0 else last - k
+
+    def sum_round(s, k):
+        for way in range(2):
+            sum_step(s, way, order(way, k))
+
+    def sum_final(s):
+        final[...] = terms[s, z].astype(jnp.float32)
+        for way in range(2):
+            land = from_right if way == 0 else from_left
+
+            @pl.when((z < last) if way == 0 else (z > 0))
+            def _():
+                line_copy(
+                    terms.at[s, z], land.at[s, z], r_send.at[way, s, z], r_recv.at[way, s, z],
+                    left if way == 0 else right,
+                ).wait_recv()
+                final[...] += land[s, z].astype(jnp.float32)
+
+        o_ref[rows_of(s)] = final[...].astype(jnp.bfloat16)
+
+    def sum_end():
+        for s in range(stripes):
+            for way in range(2):
+                for d in range(shards):
+
+                    @pl.when(sum_sent(way, d))
+                    def _():
+                        sum_copy(s, way, d).wait_send()
+
+    feature_first(0)
+    for s in range(stripes):
+        xg[z, rows_of(s)] = x_ref[rows_of(s)]
+    for hop in range(1, last):
+        feature_hop(0, hop)
+    feature_first(1)
+    feature_hop(0, last)
+    for p in range(1, stripes + 1):
+        coming = p < stripes
+        project_kv(p - 1)
+        kv_own(p - 1)
+        if coming:
+            feature_hop(p, 1)
+        project_q(p - 1)
+        if p >= 2:
+            kv_all(p - 2)
+            late(p - 2)
+        if coming:
+            feature_hop(p, 2)
+        if p >= 2:
+            project_out(p - 2)
+        kv_near(p - 1)
+        if p + 1 < stripes:
+            feature_first(p + 1)
+        if p >= 2:
+            sum_round(p - 2, 0)
+        if coming:
+            feature_hop(p, last)
+        early(p - 1)
+        kv_far(p - 1)
+        if p >= 2:
+            for k in range(1, last):
+                sum_round(p - 2, k)
+            sum_final(p - 2)
+    final_stripe = stripes - 1
+    kv_all(final_stripe)
+    late(final_stripe)
+    project_out(final_stripe)
+    for k in range(last):
+        sum_round(final_stripe, k)
+    sum_final(final_stripe)
+    feature_end()
+    for copy in sent:
+        copy.wait_send()
+    sum_end()
+
+
+def block(meta, packed, weight, out_weight, docs, shards, stripes, plane, call):
+    rows, width = packed.shape
+    head_width = weight.shape[2]
+    full = out_weight.shape[1]
+    size = rows // stripes
+    sixteen = jnp.bfloat16
+    dma = pltpu.SemaphoreType.DMA
+    return pl.pallas_call(
+        functools.partial(block_kernel, docs),
+        in_specs=[
+            pl.BlockSpec(memory_space=pltpu.SMEM),
+            pl.BlockSpec(memory_space=pltpu.VMEM),
+            pl.BlockSpec(memory_space=pl.ANY),
+            pl.BlockSpec(memory_space=pl.ANY),
+        ],
+        out_specs=pl.BlockSpec(memory_space=pltpu.VMEM),
+        out_shape=jax.ShapeDtypeStruct((rows, width), sixteen),
+        scratch_shapes=[
+            pltpu.VMEM(weight.shape, sixteen),
+            pltpu.VMEM(out_weight.shape, sixteen),
+            pltpu.VMEM((shards, rows, width), sixteen),
+            pltpu.VMEM((size, full), sixteen),
+            pltpu.VMEM((rows, head_width), sixteen),
+            pltpu.VMEM((stripes, plane, 2, size, head_width), sixteen),
+            pltpu.VMEM((stripes, size, head_width), jnp.float32),
+            pltpu.VMEM((stripes, size, head_width), jnp.float32),
+            pltpu.VMEM((size, head_width), sixteen),
+            pltpu.VMEM((stripes, shards, size, width), sixteen),
+            pltpu.VMEM((stripes, shards, size, width), sixteen),
+            pltpu.VMEM((stripes, shards, size, width), sixteen),
+            pltpu.VMEM((size, width), jnp.float32),
+            dma((4,)),
+            dma((2, stripes, shards)),
+            dma((2, stripes, shards)),
+            dma((stripes, 7)),
+            dma((stripes, 7)),
+            dma((2, stripes, shards)),
+            dma((2, stripes, shards)),
+        ],
+        compiler_params=pltpu.CompilerParams(
+            collective_id=call, has_side_effects=True, vmem_limit_bytes=VMEM_LIMIT
+        ),
+        cost_estimate=pl.CostEstimate(flops=10_000_000_000, bytes_accessed=100_000_000, transcendentals=0),
+        name="block",
+    )(meta, packed, weight, out_weight)
+
+
 def per_device(hidden, depth, qkv_weight, out_weight):
     tokens = hidden[0]
     local_len = tokens.shape[0]
@@ -306,16 +681,20 @@
     chunk_rows = ACT_DEV // chunks
     weight = jnp.transpose(qkv_weight, (1, 0, 2))
     meta = jnp.concatenate([starts[::ctx_count], me[None]]).astype(jnp.int32)
-    rows_all = [
+    fast = (docs, ctx_count) == (2, 4) and stripes >= 2 and shards >= 2
+    rows_all = [] if fast else [
         lax.all_gather(packed[c * chunk_rows : (c + 1) * chunk_rows], "tensor", axis=0) for c in range(chunks)
     ]
     kvs, backs = [], []
-    for c in range(chunks):
+    for c in range(0 if fast else chunks):
         queries, kv = project(rows_all[c], weight)
         kvs.append(gather_plane(kv, c))
         terms = attend(meta, queries, kvs, out_weight, shards, docs, chunk_stripes)
         backs.append(lax.psum_scatter(terms, "tensor", scatter_dimension=0))
-    rows_back = jnp.concatenate(backs, axis=0)
+    if fast:
+        rows_back = block(meta, packed, weight, out_weight, docs, shards, stripes, plane, 2)
+    else:
+        rows_back = jnp.concatenate(backs, axis=0)
 
     rows_back = rows_back.reshape(stripes, size, -1)
     returned = jnp.where(owned[:, 0][:, :, None], rows_back[0][None], zero)

time: 262 us -> 225 us (0.86)
  waiting for transfers between devices: 78.1 us -> 16.3 us
  Pallas kernels: 103 us -> 141 us
  between operations: 13.3 us -> 0.06 us
    pallas_call x6 -> x1, Pallas kernels: 103 us -> 141 us  [block(): pl.pallas_call(functools.partial(block_kernel, docs), in_specs=[pl.BlockS...]
    all_gather x2 -> x0, waiting for transfers between devices: 31.3 us -> none  [per_device(): lax.all_gather(packed[c * chunk_rows:(c + 1) * chunk_rows], 'tensor', axi...]
    reduce_scatter x2 -> x0, waiting for transfers between devices: 29.2 us -> none  [per_device(): backs.append(lax.psum_scatter(terms, 'tensor', scatter_dimension=0))]
  transfers between devices with their start and end apart: 5 -> 1, of which waited for: 3 -> 1; matrix products, arithmetic and copies ran while one was open for 1% -> 0% of each run, Pallas kernels for 39% -> 0%
where the time goes in v1:
time: 225 us; the launch traced here: 222 us
  Pallas kernels  141 us (63%)
  blocking collectives  29.4 us (13%)
  matrix products  20.2 us (9%)
  waiting for transfers between devices  16.3 us (7%)
  other arithmetic  6.57 us (3%)
  local copies, waits for them, and re-layouts  4.8 us (2%)
  starting transfers between devices  3.57 us (2%)
    pallas_call x1, Pallas kernels, block(): pl.pallas_call(functools.partial(block_kernel, docs), in_specs=[pl.BlockS...  141 us
    all_to_all x1, blocking collectives, per_device(): landed = lax.all_to_all(returned, PLANE, 0, 0).reshape(CAP, -1)  19.9 us
    all_to_all x1, waiting for transfers between devices, per_device(): received = lax.all_to_all(dealt.reshape(plane, size, -1), PLANE, 0, 0)  16.3 us
    dot_general x1, matrix products, per_device(): jnp.dot(onehot, tokens, preferred_element_type=jnp.float32)  10.8 us
    unnamed x1, blocking collectives  9.49 us
    dot_general x1, matrix products, per_device(): jnp.dot(spread, landed, preferred_element_type=jnp.float32)  9.37 us
  transfers between devices with their start and end apart: 1, of which 1 were waited for; matrix products, arithmetic and copies ran while one was open for 0% of the time, Pallas kernels for 0%

profile of v1, /device:TPU:0, one launch (start us, length us, event | category | flops | bytes accessed | tf_op | source)
XLA Modules:
  0.0 221.8 jit_solution(7342434936171680139)
XLA Ops:
  0.0 0.8 fusion.21
  0.8 0.6 convert_reduce_fusion
  1.4 1.2 dynamic-slice
  2.6 1.3 dynamic-update-slice
  4.0 9.5 %all-reduce = s32[8]{0:T(128)S(1)} all-reduce(s32[8]{0:T(128)S(1)} %dynamic-update-slice), channel_id=1, replica_groups=mesh['dp'=2,'ctx'=4,'tensor'=4] {'dp','ctx'}, use_global_device_ids=true, to_apply=%add | all-reduce | flops 8 | bytes 64
  13.5 0.3 reduce-window.20
  13.7 0.2 reduce-window.19
  13.9 0.1 slice.113
  14.0 0.1 reduce-window.21
  14.1 0.1 slice_reduce_fusion
  14.2 0.6 dynamic_slice.3
  14.8 0.7 fusion.18
  15.5 0.8 fusion.20
  16.2 10.8 %fusion.7 = bf16[1024,640]{1,0:T(8,128)(2,1)} fusion(bf16[1,4096,640]{2,1,0:T(8,128)(2,1)} %param.4, s32[4096]{0:T(1024)S(1)} %bitcast.88), kind=kOutput, calls=%fused_computation.9 | convolution fusion | flops 5373558784 | bytes 6569984 | tf_op jit(solution)/shard_map/dot_general | solution.py:664
  27.0 3.6 %all-to-all-start = ((bf16[8,128,640]{2,1,0:T(8,128)(2,1)}), bf16[8,128,640]{2,1,0:T(8,128)(2,1)S(1)}, u32[]{:S(2)}, u32[]{:S(2)}) async-start(bf16[8,128,640]{2,1,0:T(8,128)(2,1)} %bitcast.12), calls=%async_computation | async-start | bytes 2621440 | tf_op jit(solution)/shard_map/all_to_all | solution.py:665
  30.6 0.1 slice.89
  30.7 0.6 pad_add_fusion.meta_ref
  31.3 0.1 iota_add_fusion
  31.4 0.1 compare_and_fusion
  31.5 0.1 slice_reduce_fusion.8
  31.5 16.3 %all-to-all-done = bf16[8,128,640]{2,1,0:T(8,128)(2,1)S(1)} async-done(((bf16[8,128,640]{2,1,0:T(8,128)(2,1)}), bf16[8,128,640]{2,1,0:T(8,128)(2,1)S(1)}, u32[]{:S(2)}, u32[]{:S(2)}) %all-to-all-start) | async-done | bytes 1310752 | tf_op jit(solution)/shard_map/all_to_all | solution.py:665
  47.8 0.1 slice_bitcast_fusion.7
  48.0 1.5 fusion.16.x_ref
  49.4 140.9 %block.1 = bf16[512,640]{1,0:T(8,128)(2,1)} custom-call(s32[3]{0:T(128)} %pad_add_fusion.meta_ref, bf16[512,640]{1,0:T(8,128)(2,1)} %fusion.16.x_ref, bf16[3,2560,640]{2,1,0:T(8,128)(2,1)} %bitcast.98, bf16[640,2560]{1,0:T(8,128)(2,1)} %wo_hbm.1), custom_call_target="tpu_custom_call" | custom-call | flops 10000000000 | bytes 100000000 | tf_op jit(solution)/shard_map/block/pallas_call | solution.py:605
  190.4 1.2 fusion.23
  191.6 0.9 select_select_fusion
  192.5 19.9 %all_to_all.10 = bf16[8,128,640]{2,1,0:T(8,128)(2,1)S(1)} all-to-all(bf16[8,128,640]{2,1,0:T(8,128)(2,1)S(1)} %select_select_fusion), channel_id=1, replica_groups=mesh['dp'=2,'ctx'=4,'tensor'=4] {'dp','ctx'}, dimensions={0} | all-to-all | bytes 2621440 | tf_op jit(solution)/shard_map/all_to_all | solution.py:703
  212.4 9.4 %fusion.5 = bf16[1,4096,640]{2,1,0:T(8,128)(2,1)} fusion(bf16[1024,640]{1,0:T(8,128)(2,1)S(1)} %bitcast.85, s32[4096]{0:T(1024)S(1)} %get-tuple-element.13), kind=kOutput, calls=%fused_computation.7 | convolution fusion | flops 5375524864 | bytes 6569984 | tf_op jit(solution)/shard_map/dot_general | solution.py:705
  (4 shorter events, 0.0 us)
Async XLA Ops:
  27.0 20.8 %all-to-all-start = ((bf16[8,128,640]{2,1,0:T(8,128)(2,1)}), bf16[8,128,640]{2,1,0:T(8,128)(2,1)S(1)}, u32[]{:S(2)}, u32[]{:S(2)}) async-start(bf16[8,128,640]{2,1,0:T(8,128)(2,1)} %bitcast.12), calls=%async_computation | async-start | bytes 2621440 | tf_op jit(solution)/shard_map/all_to_all | solution.py:665

commit v2 on v1

--- a/solution.py
+++ b/solution.py
@@ -85,103 +85,6 @@
         cost_estimate=pl.CostEstimate(flops=flops, bytes_accessed=2 * weight.size, transcendentals=0),
         name="project",
     )(rows_all, weight)
-
-
-def gather_kernel(pieces, kv_ref, out_ref, send_sem, recv_sem, local_sem):
-    x, place = lax.axis_index("dp"), lax.axis_index("ctx")
-    y, core = place // 2, lax.rem(place, 2)
-    rows = kv_ref.shape[1] // pieces
-
-    def block(flip_x, flip_y, flip_core):
-        return (x ^ flip_x) * 4 + (y ^ flip_y) * 2 + (core ^ flip_core)
-
-    def device(flip_x, flip_y, flip_core):
-        return {"dp": x ^ flip_x, "ctx": (y ^ flip_y) * 2 + (core ^ flip_core)}
-
-    sibling, across_x, across_y = device(0, 0, 1), device(1, 0, 0), device(0, 1, 0)
-    barrier = pltpu.get_barrier_semaphore()
-    for target in (sibling, across_x, across_y):
-        pl.semaphore_signal(barrier, inc=1, device_id=target, device_id_type=pl.DeviceIdType.MESH)
-    pl.semaphore_wait(barrier, 3)
-
-    me = block(0, 0, 0)
-    local = pltpu.make_async_copy(kv_ref, out_ref.at[me], local_sem)
-    local.start()
-    sends = []
-
-    def send(origin, route, piece, target, own=False):
-        window = pl.ds(piece * rows, rows)
-        copy = pltpu.make_async_remote_copy(
-            src_ref=kv_ref.at[:, window] if own else out_ref.at[origin, :, window],
-            dst_ref=out_ref.at[origin, :, window],
-            send_sem=send_sem.at[route, piece],
-            recv_sem=recv_sem.at[route, piece],
-            device_id=target,
-            device_id_type=pl.DeviceIdType.MESH,
-        )
-        copy.start()
-        sends.append(copy)
-
-    def arrive(origin, route, piece):
-        window = pl.ds(piece * rows, rows)
-        pltpu.make_async_remote_copy(
-            src_ref=out_ref.at[origin, :, window],
-            dst_ref=out_ref.at[origin, :, window],
-            send_sem=send_sem.at[route, piece],
-            recv_sem=recv_sem.at[route, piece],
-            device_id=sibling,
-            device_id_type=pl.DeviceIdType.MESH,
-        ).wait_recv()
-
-    for piece in range(pieces):
-        send(me, 1, piece, across_x, True)
-        send(me, 2, piece, across_y, True)
-        send(me, 0, piece, sibling, True)
-    first = core == 0
-    onward = jnp.where(first, block(0, 1, 0), block(1, 0, 0))
-    onward_device = {
-        "dp": jnp.where(first, x ^ 1, x),
-        "ctx": jnp.where(first, place, (y ^ 1) * 2 + core),
-    }
-    for piece in range(pieces):
-        arrive(block(1, 0, 0), 1, piece)
-        arrive(block(0, 1, 0), 2, piece)
-        send(onward, 3, piece, onward_device)
-        send(block(1, 0, 0), 4, piece, sibling)
-        send(block(0, 1, 0), 5, piece, sibling)
-    for piece in range(pieces):
-        arrive(block(1, 1, 0), 3, piece)
-        send(block(1, 1, 0), 6, piece, sibling)
-    for piece in range(pieces):
-        arrive(block(0, 0, 1), 0, piece)
-        arrive(block(1, 0, 1), 4, piece)
-        arrive(block(0, 1, 1), 5, piece)
-        arrive(block(1, 1, 1), 6, piece)
-    for copy in sends:
-        copy.wait_send()
-    local.wait()
-
-
-def gather_plane(kv, call):
-    docs, ctx_count = lax.axis_size("dp"), lax.axis_size("ctx")
-    if (docs, ctx_count) != (2, 4):
-        return lax.all_gather(kv, PLANE, axis=0)
-    pieces = 8
-    plane = docs * ctx_count
-    return pl.pallas_call(
-        functools.partial(gather_kernel, pieces),
-        out_shape=jax.ShapeDtypeStruct((plane,) + kv.shape, kv.dtype),
-        in_specs=[pl.BlockSpec(memory_space=pltpu.VMEM)],
-        out_specs=pl.BlockSpec(memory_space=pl.ANY),
-        scratch_shapes=[
-            pltpu.SemaphoreType.DMA((7, pieces)),
-            pltpu.SemaphoreType.DMA((7, pieces)),
-            pltpu.SemaphoreType.DMA,
-        ],
-        compiler_params=pltpu.CompilerParams(collective_id=call, has_side_effects=True),
-        cost_estimate=pl.CostEstimate(flops=0, bytes_accessed=60_000_000, transcendentals=0),
-        name="gather_plane",
-    )(kv)
 
 
 def attend_kernel(docs, base, meta_ref, q_ref, *refs):
@@ -279,15 +182,16 @@
 
 
 def block_kernel(
-    docs, meta_ref, x_ref, w_hbm, wo_hbm, o_ref,
-    w, wo, xg, normed, query, kv, num, den, context, terms, from_right, from_left, final,
-    w_sem, a_send, a_recv, g_send, g_recv, r_send, r_recv,
+    docs, first_meta, meta_ref, deal_ref, w_hbm, wo_hbm, landed_ref,
+    received, x_ref, o_ref, returned, w, wo, xg, normed, query, kv, num, den, context, terms, from_right, from_left, final,
+    w_sem, a_send, a_recv, g_send, g_recv, r_send, r_recv, d_send, d_recv, b_send, b_recv,
 ):
     shards, rows, width = xg.shape
     stripes, plane, _, size, head_width = kv.shape
     heads = head_width // HD
     period = plane * size
     last = shards - 1
+    row = lax.broadcasted_iota(jnp.int32, (size, 1), 0)
     x, place, z = lax.axis_index("dp"), lax.axis_index("ctx"), lax.axis_index("tensor")
     y, core = place // 2, lax.rem(place, 2)
 
@@ -296,6 +200,10 @@
 
     def device(flip_x, flip_y, flip_core):
         return {"dp": x ^ flip_x, "ctx": (y ^ flip_y) * 2 + (core ^ flip_core)}
+
+    def peer(flip):
+        flips = flip // 4, (flip // 2) % 2, flip % 2
+        return block(*flips), device(*flips)
 
     me = block(0, 0, 0)
     sibling, across_x, across_y = device(0, 0, 1), device(1, 0, 0), device(0, 1, 0)
@@ -307,8 +215,8 @@
         loads[which].start()
 
     barrier = pltpu.get_barrier_semaphore()
-    for target in (sibling, across_x, across_y):
-        pl.semaphore_signal(barrier, inc=1, device_id=target, device_id_type=pl.DeviceIdType.MESH)
+    for flip in range(1, plane):
+        pl.semaphore_signal(barrier, inc=1, device_id=peer(flip)[1], device_id_type=pl.DeviceIdType.MESH)
 
     @pl.when(z > 0)
     def _():
@@ -318,10 +226,53 @@
     def _():
         pl.semaphore_signal(barrier, inc=1, device_id=right, device_id_type=pl.DeviceIdType.MESH)
 
-    pl.semaphore_wait(barrier, 3 + jnp.where(z > 0, 1, 0) + jnp.where(z < last, 1, 0))
+    pl.semaphore_wait(barrier, plane - 1 + jnp.where(z > 0, 1, 0) + jnp.where(z < last, 1, 0))
 
     def rows_of(s):
         return pl.ds(s * size, size)
+
+    def deal_copy(flip):
+        other, target = peer(flip)
+        return line_copy(deal_ref.at[other], received.at[me], d_send.at[flip], d_recv.at[flip], target)
+
+    def back_copy(flip):
+        other, target = peer(flip)
+        return line_copy(returned.at[other], landed_ref.at[me], b_send.at[flip], b_recv.at[flip], target)
+
+    far_first = (6, 7, 4, 5, 2, 3, 1)
+
+    def owned(b, s):
+        index = s * period + me * size + row
+        return (index >= meta_ref[first_meta + b]) & (index < meta_ref[first_meta + b + 1])
+
+    def deal():
+        for flip in far_first:
+            deal_copy(flip).start()
+        received[me] = deal_ref[me]
+        for flip in far_first:
+            other, target = peer(flip)
+            line_copy(deal_ref.at[other], received.at[other], d_send.at[flip], d_recv.at[flip], target).wait_recv()
+        for s in range(stripes):
+            picked = jnp.zeros((size, width), jnp.float32)
+            for b in range(plane):
+                picked = jnp.where(owned(b, s), received[b].astype(jnp.float32), picked)
+            x_ref[rows_of(s)] = picked.astype(jnp.bfloat16)
+
+    def give_back():
+        for b in range(plane):
+            picked = jnp.zeros((size, width), jnp.float32)
+            for s in range(stripes):
+                picked = jnp.where(owned(b, s), o_ref[rows_of(s)].astype(jnp.float32), picked)
+            returned[b] = picked.astype(jnp.bfloat16)
+        for flip in far_first:
+            back_copy(flip).start()
+        landed_ref[me] = returned[me]
+        for flip in far_first:
+            other, target = peer(flip)
+            line_copy(returned.at[other], landed_ref.at[other], b_send.at[flip], b_recv.at[flip], target).wait_recv()
+        for flip in far_first:
+            deal_copy(flip).wait_send()
+            back_copy(flip).wait_send()
 
     def feature_copy(s, way, hop):
         origin = z + hop if way == 0 else z - hop
@@ -443,14 +394,14 @@
         for h, value in enumerate(head_normed(part_of(0), score_scale)):
             query[rows_of(s), h * HD : (h + 1) * HD] = value
 
-    row = lax.broadcasted_iota(jnp.int32, (size, 1), 0)
     lane = lax.broadcasted_iota(jnp.int32, (1, period), 1)
 
     def begin_of(s):
         q_index = s * period + me * size + row
         begin = jnp.zeros((size, 1), jnp.int32)
         for d in range(docs):
-            begin = jnp.where(q_index >= meta_ref[d], meta_ref[d], begin)
+            at = first_meta + d * (plane // docs)
+            begin = jnp.where(q_index >= meta_ref[at], meta_ref[at], begin)
         return begin
 
     def attend(s, steps):
@@ -504,25 +455,25 @@
     def sum_sent(way, d):
         return (z > d) if way == 0 else (z < d)
 
-    def sum_step(s, way, d):
-        inner = (z < last) if way == 0 else (z > 0)
-        land = from_right if way == 0 else from_left
-
-        @pl.when(sum_sent(way, d) & inner)
-        def _():
-            sum_copy(s, way, d).wait_recv()
-            terms[s, d] = (terms[s, d].astype(jnp.float32) + land[s, d].astype(jnp.float32)).astype(jnp.bfloat16)
-
-        @pl.when(sum_sent(way, d))
-        def _():
-            sum_copy(s, way, d).start()
-
-    def order(way, k):
-        return k if way == 0 else last - k
-
-    def sum_round(s, k):
+    def sum_first(s):
         for way in range(2):
-            sum_step(s, way, order(way, k))
+            for k in range(last):
+
+                @pl.when(z == (last if way == 0 else 0))
+                def _():
+                    sum_copy(s, way, k if way == 0 else last - k).start()
+
+    def sum_round(s, r):
+        for way in range(2):
+            land = from_right if way == 0 else from_left
+            k = r - last + z if way == 0 else r - z
+            d = k if way == 0 else last - k
+
+            @pl.when((k >= 0) & ((z < last) if way == 0 else (z > 0)))
+            def _():
+                sum_copy(s, way, d).wait_recv()
+                terms[s, d] = (terms[s, d].astype(jnp.float32) + land[s, d].astype(jnp.float32)).astype(jnp.bfloat16)
+                sum_copy(s, way, d).start()
 
     def sum_final(s):
         final[...] = terms[s, z].astype(jnp.float32)
@@ -531,10 +482,7 @@
 
             @pl.when((z < last) if way == 0 else (z > 0))
             def _():
-                line_copy(
-                    terms.at[s, z], land.at[s, z], r_send.at[way, s, z], r_recv.at[way, s, z],
-                    left if way == 0 else right,
-                ).wait_recv()
+                sum_copy(s, way, z).wait_recv()
                 final[...] += land[s, z].astype(jnp.float32)
 
         o_ref[rows_of(s)] = final[...].astype(jnp.bfloat16)
@@ -548,62 +496,67 @@
                     def _():
                         sum_copy(s, way, d).wait_send()
 
+    deal()
     feature_first(0)
     for s in range(stripes):
         xg[z, rows_of(s)] = x_ref[rows_of(s)]
-    for hop in range(1, last):
+    feature_hop(0, 1)
+    feature_first(1)
+    for hop in range(2, last + 1):
         feature_hop(0, hop)
-    feature_first(1)
-    feature_hop(0, last)
-    for p in range(1, stripes + 1):
-        coming = p < stripes
-        project_kv(p - 1)
-        kv_own(p - 1)
+    for p in range(stripes + 2):
+        here, coming = p < stripes, p + 1 < stripes
+        before, older, oldest = 0 <= p - 1 < stripes, 0 <= p - 2 < stripes, 0 <= p - 3 < stripes
+        if here:
+            project_kv(p)
+            kv_own(p)
+        if before:
+            kv_near(p - 1)
+        if here:
+            project_q(p)
+        if oldest:
+            sum_final(p - 3)
         if coming:
-            feature_hop(p, 1)
-        project_q(p - 1)
-        if p >= 2:
-            kv_all(p - 2)
-            late(p - 2)
+            feature_hop(p + 1, 1)
+            if p + 2 < stripes:
+                feature_first(p + 2)
+        if before:
+            kv_far(p - 1)
+        if older:
+            sum_round(p - 2, 1)
+        if before:
+            kv_all(p - 1)
         if coming:
-            feature_hop(p, 2)
-        if p >= 2:
-            project_out(p - 2)
-        kv_near(p - 1)
-        if p + 1 < stripes:
-            feature_first(p + 1)
-        if p >= 2:
-            sum_round(p - 2, 0)
+            feature_hop(p + 1, 2)
+        if before:
+            late(p - 1)
+            project_out(p - 1)
+            sum_first(p - 1)
+        if older:
+            for r in range(2, last):
+                sum_round(p - 2, r)
+        if here:
+            early(p)
         if coming:
-            feature_hop(p, last)
-        early(p - 1)
-        kv_far(p - 1)
-        if p >= 2:
-            for k in range(1, last):
-                sum_round(p - 2, k)
-            sum_final(p - 2)
-    final_stripe = stripes - 1
-    kv_all(final_stripe)
-    late(final_stripe)
-    project_out(final_stripe)
-    for k in range(last):
-        sum_round(final_stripe, k)
-    sum_final(final_stripe)
+            for hop in range(3, last + 1):
+                feature_hop(p + 1, hop)
+    sum_final(stripes - 1)
+    give_back()
     feature_end()
     for copy in sent:
         copy.wait_send()
     sum_end()
 
 
-def block(meta, packed, weight, out_weight, docs, shards, stripes, plane, call):
-    rows, width = packed.shape
+def block(meta, first_meta, dealt, weight, out_weight, docs, shards, stripes, call):
+    plane, size, width = dealt.shape
+    rows = stripes * size
     head_width = weight.shape[2]
     full = out_weight.shape[1]
-    size = rows // stripes
     sixteen = jnp.bfloat16
     dma = pltpu.SemaphoreType.DMA
     return pl.pallas_call(
-        functools.partial(block_kernel, docs),
+        functools.partial(block_kernel, docs, first_meta),
         in_specs=[
             pl.BlockSpec(memory_space=pltpu.SMEM),
             pl.BlockSpec(memory_space=pltpu.VMEM),
@@ -611,8 +564,12 @@
             pl.BlockSpec(memory_space=pl.ANY),
         ],
         out_specs=pl.BlockSpec(memory_space=pltpu.VMEM),
-        out_shape=jax.ShapeDtypeStruct((rows, width), sixteen),
+        out_shape=jax.ShapeDtypeStruct((plane, size, width), sixteen),
         scratch_shapes=[
+            pltpu.VMEM((plane, size, width), sixteen),
+            pltpu.VMEM((rows, width), sixteen),
+            pltpu.VMEM((rows, width), sixteen),
+            pltpu.VMEM((plane, size, width), sixteen),
             pltpu.VMEM(weight.shape, sixteen),
             pltpu.VMEM(out_weight.shape, sixteen),
             pltpu.VMEM((shards, rows, width), sixteen),
@@ -633,13 +590,207 @@
             dma((stripes, 7)),
             dma((2, stripes, shards)),
             dma((2, stripes, shards)),
+            dma((plane,)),
+            dma((plane,)),
+            dma((plane,)),
+            dma((plane,)),
         ],
         compiler_params=pltpu.CompilerParams(
             collective_id=call, has_side_effects=True, vmem_limit_bytes=VMEM_LIMIT
         ),
         cost_estimate=pl.CostEstimate(flops=10_000_000_000, bytes_accessed=100_000_000, transcendentals=0),
         name="block",
-    )(meta, packed, weight, out_weight)
+    )(meta, dealt, weight, out_weight)
+
+
+LINES = 32
+
+
+def count_kernel(depth_ref, place_ref, info_ref, mine, landed, send_sem, recv_sem):
+    plane = landed.shape[0]
+    lines, lanes = depth_ref.shape
+    ctx_count = lax.axis_size("ctx")
+    x, place = lax.axis_index("dp"), lax.axis_index("ctx")
+    me = x * ctx_count + place
+
+    def device(flip):
+        return {"dp": x ^ (flip // ctx_count), "ctx": place ^ (flip % ctx_count)}
+
+    barrier = pltpu.get_barrier_semaphore()
+    for flip in range(1, plane):
+        pl.semaphore_signal(barrier, inc=1, device_id=device(flip), device_id_type=pl.DeviceIdType.MESH)
+    active = depth_ref[...] >= RECURSION
+    ones = jnp.where(active, 1.0, 0.0)
+    total = jnp.sum(jnp.sum(ones, axis=1, keepdims=True), axis=0, keepdims=True)
+    mine[...] = jnp.broadcast_to(total, mine.shape).astype(jnp.int32)
+    pl.semaphore_wait(barrier, plane - 1)
+
+    def copy(flip, slot):
+        return line_copy(mine, landed.at[slot], send_sem.at[flip], recv_sem.at[flip], device(flip))
+
+    for flip in range(1, plane):
+        copy(flip, me).start()
+    landed[me] = mine[...]
+    upto = lax.broadcasted_iota(jnp.int32, (lanes, lanes), 0) <= lax.broadcasted_iota(jnp.int32, (lanes, lanes), 1)
+    inside = jnp.dot(
+        ones.astype(jnp.bfloat16), jnp.where(upto, 1.0, 0.0).astype(jnp.bfloat16), preferred_element_type=jnp.float32
+    )
+    ahead = lax.broadcasted_iota(jnp.int32, (lines, lines), 1) < lax.broadcasted_iota(jnp.int32, (lines, lines), 0)
+    line_total = jnp.broadcast_to(inside[:, lanes - 1 :], (lines, lanes))
+    before = jnp.dot(
+        jnp.where(ahead, 1.0, 0.0).astype(jnp.bfloat16),
+        line_total.astype(jnp.bfloat16),
+        preferred_element_type=jnp.float32,
+    )
+    for flip in range(1, plane):
+        copy(flip, me ^ flip).wait_recv()
+    start = jnp.zeros((1, lanes), jnp.int32)
+    running = jnp.zeros((1, lanes), jnp.int32)
+    for b in range(plane):
+        info_ref[lines + b : lines + b + 1] = running
+        count = landed[b, 0:1]
+        start = start + jnp.where(me > b, count, 0)
+        running = running + count
+    for b in range(plane, info_ref.shape[0] - lines):
+        info_ref[lines + b : lines + b + 1] = running
+    base = (start & (CAP - 1)) + before.astype(jnp.int32)
+    info_ref[:lines] = base
+    place_ref[...] = jnp.where(active, base + inside.astype(jnp.int32) - 1, -1)
+    for flip in range(1, plane):
+        copy(flip, me).wait_send()
+
+
+def count(depth, plane, call):
+    lines = LINES
+    lanes = depth.shape[0] // lines
+    whole = jnp.int32
+    return pl.pallas_call(
+        count_kernel,
+        in_specs=[pl.BlockSpec(memory_space=pltpu.VMEM)],
+        out_specs=[pl.BlockSpec(memory_space=pltpu.VMEM)] * 2,
+        out_shape=[
+            jax.ShapeDtypeStruct((lines, lanes), whole),
+            jax.ShapeDtypeStruct((lines + 16, lanes), whole),
+        ],
+        scratch_shapes=[
+            pltpu.VMEM((8, lanes), whole),
+            pltpu.VMEM((plane, 8, lanes), whole),
+            pltpu.SemaphoreType.DMA((plane,)),
+            pltpu.SemaphoreType.DMA((plane,)),
+        ],
+        compiler_params=pltpu.CompilerParams(collective_id=call, has_side_effects=True),
+        name="count",
+    )(depth.reshape(lines, lanes))
+
+
+ALIGN = 16
+GROUP = 2
+LOADS = 8
+
+
+def onehot_of(place_ref, at, floor, window):
+    wanted = jnp.concatenate([place_ref[pl.ds(at + i, 1), :] for i in range(GROUP)], axis=1)
+    spot = lax.broadcasted_iota(jnp.int32, (window, wanted.shape[1]), 0)
+    return jnp.where(spot + floor == wanted, 1.0, 0.0).astype(jnp.bfloat16)
+
+
+def compact_kernel(info_ref, place_ref, tokens_hbm, out_ref, tokens, buffer, sems):
+    lines, lanes = place_ref.shape
+    block_rows = GROUP * lanes
+    window = block_rows + ALIGN
+    chunk = tokens.shape[0] // LOADS
+    loads = []
+    for i in range(LOADS):
+        rows = pl.ds(i * chunk, chunk)
+        loads.append(pltpu.make_async_copy(tokens_hbm.at[rows], tokens.at[rows], sems.at[i]))
+        loads[-1].start()
+    start = info_ref[0]
+    edge = lax.broadcasted_iota(jnp.int32, (ALIGN, 1), 0)
+    for i in range(lines // GROUP):
+        if (i * block_rows) % chunk == 0:
+            loads[i * block_rows // chunk].wait()
+        base = info_ref[i * GROUP]
+        floor = pl.multiple_of(base - lax.rem(base, ALIGN), ALIGN)
+        spread = onehot_of(place_ref, i * GROUP, floor, window)
+        rows = tokens[i * block_rows : (i + 1) * block_rows]
+        found = jnp.dot(spread, rows, preferred_element_type=jnp.float32)
+        old = buffer[pl.ds(floor, ALIGN)].astype(jnp.float32)
+        seam = jnp.where(edge < base - floor, old, found[:ALIGN])
+        buffer[pl.ds(floor, ALIGN)] = seam.astype(jnp.bfloat16)
+        buffer[pl.ds(floor + ALIGN, block_rows)] = found[ALIGN:].astype(jnp.bfloat16)
+    plane, size, _ = out_ref.shape
+    for b in range(plane):
+        spot = b * size + lax.broadcasted_iota(jnp.int32, (size, 1), 0)
+        low = buffer[b * size : (b + 1) * size].astype(jnp.float32)
+        high = buffer[CAP + b * size : CAP + (b + 1) * size].astype(jnp.float32)
+        out_ref[b] = jnp.where(spot >= start, low, high).astype(jnp.bfloat16)
+
+
+def compact(info, places, tokens, plane):
+    lines, lanes = places.shape
+    width = tokens.shape[1]
+    return pl.pallas_call(
+        compact_kernel,
+        in_specs=[
+            pl.BlockSpec(memory_space=pltpu.SMEM),
+            pl.BlockSpec(memory_space=pltpu.VMEM),
+            pl.BlockSpec(memory_space=pl.ANY),
+        ],
+        out_specs=pl.BlockSpec(memory_space=pltpu.VMEM),
+        out_shape=jax.ShapeDtypeStruct((plane, CAP // plane, width), tokens.dtype),
+        scratch_shapes=[
+            pltpu.VMEM(tokens.shape, tokens.dtype),
+            pltpu.VMEM((2 * CAP + GROUP * lanes + ALIGN, width), tokens.dtype),
+            pltpu.SemaphoreType.DMA((LOADS,)),
+        ],
+        compiler_params=pltpu.CompilerParams(vmem_limit_bytes=VMEM_LIMIT),
+        name="compact",
+    )(info, places, tokens)
+
+
+def unpack_kernel(parts, info_ref, place_ref, landed_ref, out_ref, buffer):
+    step = pl.program_id(0)
+    _, lanes = place_ref.shape
+    block_rows = GROUP * lanes
+    window = block_rows + ALIGN
+
+    @pl.when(step == 0)
+    def _():
+        buffer[:CAP] = landed_ref[...]
+        buffer[CAP:] = landed_ref[: buffer.shape[0] - CAP]
+
+    for i in range(parts):
+        line = (step * parts + i) * GROUP
+        base = info_ref[line]
+        floor = base - lax.rem(base, ALIGN)
+        spread = onehot_of(place_ref, line, floor, window)
+        rows = buffer[pl.ds(pl.multiple_of(lax.rem(floor, CAP), ALIGN), window)]
+        out_ref[i * block_rows : (i + 1) * block_rows] = lax.dot_general(
+            spread, rows, (((0,), (0,)), ((), ())), preferred_element_type=jnp.float32
+        ).astype(jnp.bfloat16)
+
+
+def unpack(info, places, landed, length):
+    lines, lanes = places.shape
+    width = landed.shape[1]
+    steps = 8
+    parts = lines // GROUP // steps
+    return pl.pallas_call(
+        functools.partial(unpack_kernel, parts),
+        grid_spec=pltpu.PrefetchScalarGridSpec(
+            num_scalar_prefetch=1,
+            grid=(steps,),
+            in_specs=[
+                pl.BlockSpec((lines, lanes), lambda i, m: (0, 0)),
+                pl.BlockSpec(landed.shape, lambda i, m: (0, 0)),
+            ],
+            out_specs=pl.BlockSpec((length // steps, width), lambda i, m: (i, 0)),
+            scratch_shapes=[pltpu.VMEM((CAP + GROUP * lanes + ALIGN, width), landed.dtype)],
+        ),
+        out_shape=jax.ShapeDtypeStruct((length, width), landed.dtype),
+        compiler_params=pltpu.CompilerParams(vmem_limit_bytes=VMEM_LIMIT),
+        name="unpack",
+    )(info, places, landed)
 
 
 def per_device(hidden, depth, qkv_weight, out_weight):
@@ -652,6 +803,14 @@
     me = lax.axis_index("dp") * ctx_count + lax.axis_index("ctx")
     size = CAP // plane
     stripes = ACT_DEV // size
+
+    if (docs, ctx_count) == (2, 4) and local_len % (LINES * 128) == 0 and stripes >= 2 and shards >= 2:
+        places, info = count(depth[0], plane, 0)
+        info = info[:, 0]
+        dealt = compact(info, places, tokens, plane)
+        weight = jnp.transpose(qkv_weight, (1, 0, 2))
+        landed = block(info, LINES, dealt, weight, out_weight, docs, shards, stripes, 1)
+        return unpack(info, places, landed.reshape(CAP, -1), local_len)[None]
 
     active = depth[0] >= RECURSION
     ones = active.astype(jnp.int32)
@@ -681,20 +840,16 @@
     chunk_rows = ACT_DEV // chunks
     weight = jnp.transpose(qkv_weight, (1, 0, 2))
     meta = jnp.concatenate([starts[::ctx_count], me[None]]).astype(jnp.int32)
-    fast = (docs, ctx_count) == (2, 4) and stripes >= 2 and shards >= 2
-    rows_all = [] if fast else [
+    rows_all = [
         lax.all_gather(packed[c * chunk_rows : (c + 1) * chunk_rows], "tensor", axis=0) for c in range(chunks)
     ]
     kvs, backs = [], []
-    for c in range(0 if fast else chunks):
+    for c in range(chunks):
         queries, kv = project(rows_all[c], weight)
-        kvs.append(gather_plane(kv, c))
+        kvs.append(lax.all_gather(kv, PLANE, axis=0))
         terms = attend(meta, queries, kvs, out_weight, shards, docs, chunk_stripes)
         backs.append(lax.psum_scatter(terms, "tensor", scatter_dimension=0))
-    if fast:
-        rows_back = block(meta, packed, weight, out_weight, docs, shards, stripes, plane, 2)
-    else:
-        rows_back = jnp.concatenate(backs, axis=0)
+    rows_back = jnp.concatenate(backs, axis=0)
 
     rows_back = rows_back.reshape(stripes, size, -1)
     returned = jnp.where(owned[:, 0][:, :, None], rows_back[0][None], zero)

time: 225 us -> 186 us (0.83); the launches traced: 222 us -> 186 us
  Pallas kernels: 141 us -> 184 us
  blocking collectives: 29.4 us -> 0 us
  matrix products: 20.2 us -> 0 us
  waiting for transfers between devices: 16.3 us -> 0 us
  other arithmetic: 6.57 us -> 0 us
  starting transfers between devices: 3.57 us -> 0 us
  local copies, waits for them, and re-layouts: 4.8 us -> 1.38 us
    pallas_call x1 -> x4, Pallas kernels: 141 us -> 184 us  [the longest x1 161 us: block(): pl.pallas_call(functools.partial(block_kernel, docs, first_meta), in_spec...]
    dot_general x2 -> x0, matrix products: 20.2 us -> none  [the longest x1 10.8 us: per_device(): jnp.dot(onehot, tokens, preferred_element_type=jnp.float32)]
    all_to_all x1 -> x0, blocking collectives: 19.9 us -> none  [per_device(): landed = lax.all_to_all(returned, PLANE, 0, 0).reshape(CAP, -1)]
    all_to_all x1 -> x0, waiting for transfers between devices: 16.3 us -> none  [per_device(): received = lax.all_to_all(dealt.reshape(plane, size, -1), PLANE, 0, 0)]
    unnamed x1 -> x0, blocking collectives: 9.49 us -> none
    select_n x4 -> x0, other arithmetic: 3.88 us -> none  [the longest x2 1.48 us: per_device(): slot = jnp.where(active, lax.rem(starts[me] + rank, CAP), -1)]
    all_to_all x1 -> x0, starting transfers between devices: 3.57 us -> none  [per_device(): received = lax.all_to_all(dealt.reshape(plane, size, -1), PLANE, 0, 0)]
    unnamed x3 -> x0, local copies, waits for them, and re-layouts: 2.54 us -> none
  transfers between devices with their start and end apart: 1 -> 0, of which waited for: 1 -> 0; matrix products, arithmetic and copies ran while one was open for 0% -> 0% of each run, Pallas kernels for 0% -> 0%
where the time goes in v2:
time: 186 us
  Pallas kernels  184 us (99%)
    pallas_call x1, Pallas kernels, block(): pl.pallas_call(functools.partial(block_kernel, docs, first_meta), in_spec...  161 us
    pallas_call x1, Pallas kernels, unpack(): pl.pallas_call(functools.partial(unpack_kernel, parts), grid_spec=pltpu.P...  8.38 us
    pallas_call x1, Pallas kernels, count(): pl.pallas_call(count_kernel, in_specs=[pl.BlockSpec(memory_space=pltpu.VM...  7.66 us
    pallas_call x1, Pallas kernels, compact(): pl.pallas_call(compact_kernel, in_specs=[pl.BlockSpec(memory_space=pltpu....  6.77 us

profile of v2, /device:TPU:0, one launch (start us, length us, event | category | flops | bytes accessed | tf_op | source)
XLA Modules:
  0.0 185.6 jit_solution(505012830226244418)
XLA Ops:
  0.0 7.7 %count.1 = (s32[32,128]{1,0:T(8,128)}, s32[48,128]{1,0:T(8,128)}) custom-call(s32[32,128]{1,0:T(8,128)} %bitcast.7), custom_call_target="tpu_custom_call" | custom-call | tf_op jit(solution)/shard_map/count/pallas_call | solution.py:667
  7.7 1.4 slice_reduce_fusion.info_ref.meta_ref
  9.0 6.8 %compact.1.deal_ref = bf16[8,128,640]{2,1,0:T(8,128)(2,1)} custom-call(s32[48]{0:T(128)} %slice_reduce_fusion.info_ref.meta_ref, s32[32,128]{1,0:T(8,128)} %get-tuple-element.8.place_ref, bf16[4096,640]{1,0:T(8,128)(2,1)} %bitcast.5), custom_call_target="tpu_custom_call" | custom-call | tf_op jit(solution)/shard_map/compact/pallas_call | solution.py:732
  15.8 161.4 %block.1 = bf16[8,128,640]{2,1,0:T(8,128)(2,1)} custom-call(s32[48]{0:T(128)} %slice_reduce_fusion.info_ref.meta_ref, bf16[8,128,640]{2,1,0:T(8,128)(2,1)} %compact.1.deal_ref, bf16[3,2560,640]{2,1,0:T(8,128)(2,1)} %bitcast.8, bf16[640,2560]{1,0:T(8,128)(2,1)} %wo_hbm.1), custom_call_target="tpu_custom_call" | custom-call | flops 10000000000 | bytes 100000000 | tf_op jit(solution)/shard_map/block/pallas_call | solution.py:558
  177.2 8.4 %unpack.1 = bf16[4096,640]{1,0:T(8,128)(2,1)} custom-call(s32[48]{0:T(128)} %slice_reduce_fusion.info_ref.meta_ref, s32[32,128]{1,0:T(8,128)} %get-tuple-element.8.place_ref, bf16[1024,640]{1,0:T(8,128)(2,1)} %bitcast.6), custom_call_target="tpu_custom_call" | custom-call | tf_op jit(solution)/shard_map/unpack/pallas_call | solution.py:778

commit v3 on v2

--- a/solution.py
+++ b/solution.py
@@ -170,6 +170,88 @@
     )(meta, queries, *operands)
 
 
+ORDER = (
+    ("first", 0),
+    ("first", 1),
+    ("hop", 0, 1),
+    ("hop", 0, 2),
+    ("hop", 0, 3),
+    ("pkv", 0),
+    ("hop", 1, 1),
+    ("own", 0),
+    ("pq", 0),
+    ("first", 2),
+    ("near", 0, 0),
+    ("hop", 1, 2),
+    ("near", 0, 1),
+    ("hop", 1, 3),
+    ("hop", 2, 1),
+    ("pkv", 1),
+    ("first", 3),
+    ("far", 0, 0),
+    ("own", 1),
+    ("hop", 2, 2),
+    ("far", 0, 1),
+    ("pq", 1),
+    ("near", 1, 0),
+    ("all", 0),
+    ("late", 0),
+    ("hop", 3, 1),
+    ("out", 0),
+    ("near", 1, 1),
+    ("rfirst", 0),
+    ("hop", 2, 3),
+    ("pkv", 2),
+    ("own", 2),
+    ("pq", 2),
+    ("far", 1, 0),
+    ("early", 2, 0),
+    ("early", 1, 0),
+    ("far", 1, 1),
+    ("all", 1),
+    ("hop", 3, 2),
+    ("near", 2, 0),
+    ("late", 1),
+    ("hop", 3, 3),
+    ("out", 1),
+    ("rfirst", 1),
+    ("round", 0, 1),
+    ("pkv", 3),
+    ("near", 2, 1),
+    ("pq", 3),
+    ("own", 3),
+    ("far", 2, 0),
+    ("early", 2, 1),
+    ("round", 0, 2),
+    ("far", 2, 1),
+    ("early", 3, 0),
+    ("all", 2),
+    ("late", 2),
+    ("round", 1, 1),
+    ("out", 2),
+    ("round", 1, 2),
+    ("rfirst", 2),
+    ("near", 3, 0),
+    ("near", 3, 1),
+    ("final", 0),
+    ("round", 2, 1),
+    ("early", 3, 1),
+    ("far", 3, 0),
+    ("far", 3, 1),
+    ("early", 3, 2),
+    ("round", 2, 2),
+    ("all", 3),
+    ("final", 1),
+    ("late", 3),
+    ("out", 3),
+    ("rfirst", 3),
+    ("round", 3, 1),
+    ("round", 3, 2),
+    ("final", 2),
+    ("final", 3),
+)
+
+
 def line_copy(src, dst, send_sem, recv_sem, to):
     return pltpu.make_async_remote_copy(
         src_ref=src,
@@ -243,7 +325,7 @@
 
     def owned(b, s):
         index = s * period + me * size + row
-        return (index >= meta_ref[first_meta + b]) & (index < meta_ref[first_meta + b + 1])
+        return (index >= meta_ref[first_meta + b, 0]) & (index < meta_ref[first_meta + b + 1, 0])
 
     def deal():
         for flip in far_first:
@@ -318,43 +400,47 @@
 
     first = core == 0
     onward = jnp.where(first, block(0, 1, 0), block(1, 0, 0))
+    other = jnp.where(first, block(1, 0, 0), block(0, 1, 0))
     onward_device = {
         "dp": jnp.where(first, x ^ 1, x),
         "ctx": jnp.where(first, place, (y ^ 1) * 2 + core),
     }
     sent = []
 
-    def kv_send(s, origin, route, target):
-        copy = line_copy(kv.at[s, origin], kv.at[s, origin], g_send.at[s, route], g_recv.at[s, route], target)
+    def kv_send(s, half, origin, route, target):
+        piece = kv.at[s, origin, half]
+        copy = line_copy(piece, piece, g_send.at[s, half, route], g_recv.at[s, half, route], target)
         copy.start()
         sent.append(copy)
 
-    def kv_arrive(s, origin, route):
-        line_copy(
-            kv.at[s, origin], kv.at[s, origin], g_send.at[s, route], g_recv.at[s, route], sibling
-        ).wait_recv()
+    def kv_arrive(s, half, origin, route):
+        piece = kv.at[s, origin, half]
+        line_copy(piece, piece, g_send.at[s, half, route], g_recv.at[s, half, route], sibling).wait_recv()
 
     def kv_own(s):
-        kv_send(s, me, 1, across_x)
-        kv_send(s, me, 2, across_y)
-        kv_send(s, me, 0, sibling)
-
-    def kv_near(s):
-        kv_arrive(s, block(1, 0, 0), 1)
-        kv_arrive(s, block(0, 1, 0), 2)
-        kv_send(s, onward, 3, onward_device)
-        kv_send(s, block(1, 0, 0), 4, sibling)
-        kv_send(s, block(0, 1, 0), 5, sibling)
-
-    def kv_far(s):
-        kv_arrive(s, block(1, 1, 0), 3)
-        kv_send(s, block(1, 1, 0), 6, sibling)
+        for half in range(2):
+            kv_send(s, half, me, 1, across_x)
+            kv_send(s, half, me, 2, across_y)
+        for half in range(2):
+            kv_send(s, half, me, 0, sibling)
+
+    def kv_near(s, half):
+        kv_arrive(s, half, onward, jnp.where(first, 2, 1))
+        kv_send(s, half, onward, 3, onward_device)
+        kv_send(s, half, onward, jnp.where(first, 5, 4), sibling)
+        kv_arrive(s, half, other, jnp.where(first, 1, 2))
+        kv_send(s, half, other, jnp.where(first, 4, 5), sibling)
+
+    def kv_far(s, half):
+        kv_arrive(s, half, block(1, 1, 0), 3)
+        kv_send(s, half, block(1, 1, 0), 6, sibling)
 
     def kv_all(s):
-        kv_arrive(s, block(0, 0, 1), 0)
-        kv_arrive(s, block(1, 0, 1), 4)
-        kv_arrive(s, block(0, 1, 1), 5)
-        kv_arrive(s, block(1, 1, 1), 6)
+        for half in range(2):
+            kv_arrive(s, half, block(0, 0, 1), 0)
+            kv_arrive(s, half, block(1, 0, 1), 4)
+            kv_arrive(s, half, block(0, 1, 1), 5)
+            kv_arrive(s, half, block(1, 1, 1), 6)
 
     def normalize(s):
         total = jnp.zeros((size, 1), jnp.float32)
@@ -401,7 +487,7 @@
         begin = jnp.zeros((size, 1), jnp.int32)
         for d in range(docs):
             at = first_meta + d * (plane // docs)
-            begin = jnp.where(q_index >= meta_ref[at], meta_ref[at], begin)
+            begin = jnp.where(q_index >= meta_ref[at, 0], meta_ref[at, 0], begin)
         return begin
 
     def attend(s, steps):
@@ -431,9 +517,8 @@
 
         lax.fori_loop(0, heads, one_head, 0)
 
-    def early(s):
-        if s > 0:
-            attend(s, list(range(s)))
+    def early(s, t):
+        attend(s, [t])
 
     def late(s):
         attend(s, [s])
@@ -497,50 +582,26 @@
                         sum_copy(s, way, d).wait_send()
 
     deal()
-    feature_first(0)
     for s in range(stripes):
         xg[z, rows_of(s)] = x_ref[rows_of(s)]
-    feature_hop(0, 1)
-    feature_first(1)
-    for hop in range(2, last + 1):
-        feature_hop(0, hop)
-    for p in range(stripes + 2):
-        here, coming = p < stripes, p + 1 < stripes
-        before, older, oldest = 0 <= p - 1 < stripes, 0 <= p - 2 < stripes, 0 <= p - 3 < stripes
-        if here:
-            project_kv(p)
-            kv_own(p)
-        if before:
-            kv_near(p - 1)
-        if here:
-            project_q(p)
-        if oldest:
-            sum_final(p - 3)
-        if coming:
-            feature_hop(p + 1, 1)
-            if p + 2 < stripes:
-                feature_first(p + 2)
-        if before:
-            kv_far(p - 1)
-        if older:
-            sum_round(p - 2, 1)
-        if before:
-            kv_all(p - 1)
-        if coming:
-            feature_hop(p + 1, 2)
-        if before:
-            late(p - 1)
-            project_out(p - 1)
-            sum_first(p - 1)
-        if older:
-            for r in range(2, last):
-                sum_round(p - 2, r)
-        if here:
-            early(p)
-        if coming:
-            for hop in range(3, last + 1):
-                feature_hop(p + 1, hop)
-    sum_final(stripes - 1)
+    steps = {
+        "first": feature_first,
+        "hop": feature_hop,
+        "pkv": project_kv,
+        "pq": project_q,
+        "own": kv_own,
+        "near": kv_near,
+        "far": kv_far,
+        "all": kv_all,
+        "early": early,
+        "late": late,
+        "out": project_out,
+        "rfirst": sum_first,
+        "round": sum_round,
+        "final": sum_final,
+    }
+    for name, *at in ORDER:
+        steps[name](*at)
     give_back()
     feature_end()
     for copy in sent:
@@ -586,8 +647,8 @@
             dma((4,)),
             dma((2, stripes, shards)),
             dma((2, stripes, shards)),
-            dma((stripes, 7)),
-            dma((stripes, 7)),
+            dma((stripes, 2, 7)),
+            dma((stripes, 2, 7)),
             dma((2, stripes, shards)),
             dma((2, stripes, shards)),
             dma((plane,)),
@@ -704,12 +765,12 @@
         rows = pl.ds(i * chunk, chunk)
         loads.append(pltpu.make_async_copy(tokens_hbm.at[rows], tokens.at[rows], sems.at[i]))
         loads[-1].start()
-    start = info_ref[0]
+    start = info_ref[0, 0]
     edge = lax.broadcasted_iota(jnp.int32, (ALIGN, 1), 0)
     for i in range(lines // GROUP):
         if (i * block_rows) % chunk == 0:
             loads[i * block_rows // chunk].wait()
-        base = info_ref[i * GROUP]
+        base = info_ref[i * GROUP, 0]
         floor = pl.multiple_of(base - lax.rem(base, ALIGN), ALIGN)
         spread = onehot_of(place_ref, i * GROUP, floor, window)
         rows = tokens[i * block_rows : (i + 1) * block_rows]
@@ -748,46 +809,49 @@
     )(info, places, tokens)
 
 
-def unpack_kernel(parts, info_ref, place_ref, landed_ref, out_ref, buffer):
-    step = pl.program_id(0)
-    _, lanes = place_ref.shape
-    block_rows = GROUP * lanes
-    window = block_rows + ALIGN
-
-    @pl.when(step == 0)
-    def _():
-        buffer[:CAP] = landed_ref[...]
-        buffer[CAP:] = landed_ref[: buffer.shape[0] - CAP]
-
-    for i in range(parts):
-        line = (step * parts + i) * GROUP
-        base = info_ref[line]
+def unpack_kernel(info_ref, place_ref, landed_ref, out_hbm, buffer, columns, out, sems):
+    lines, lanes = place_ref.shape
+    window = 2 * lanes
+    buffer[:CAP] = landed_ref[...]
+    buffer[CAP:] = landed_ref[: buffer.shape[0] - CAP]
+    columns[...] = jnp.transpose(place_ref[...])
+    spot = lax.broadcasted_iota(jnp.int32, (lanes, window), 1)
+    chunk = out.shape[0] // LOADS
+    stores = []
+    for i in range(lines):
+        base = info_ref[i, 0]
         floor = base - lax.rem(base, ALIGN)
-        spread = onehot_of(place_ref, line, floor, window)
+        spread = jnp.where(columns[:, i : i + 1] - floor == spot, 1.0, 0.0).astype(jnp.bfloat16)
         rows = buffer[pl.ds(pl.multiple_of(lax.rem(floor, CAP), ALIGN), window)]
-        out_ref[i * block_rows : (i + 1) * block_rows] = lax.dot_general(
-            spread, rows, (((0,), (0,)), ((), ())), preferred_element_type=jnp.float32
-        ).astype(jnp.bfloat16)
+        out[i * lanes : (i + 1) * lanes] = jnp.dot(spread, rows, preferred_element_type=jnp.float32).astype(
+            jnp.bfloat16
+        )
+        if (i + 1) * lanes % chunk == 0:
+            at = pl.ds((i + 1) * lanes - chunk, chunk)
+            stores.append(pltpu.make_async_copy(out.at[at], out_hbm.at[at], sems.at[len(stores)]))
+            stores[-1].start()
+    for store in stores:
+        store.wait()
 
 
 def unpack(info, places, landed, length):
     lines, lanes = places.shape
     width = landed.shape[1]
-    steps = 8
-    parts = lines // GROUP // steps
     return pl.pallas_call(
-        functools.partial(unpack_kernel, parts),
-        grid_spec=pltpu.PrefetchScalarGridSpec(
-            num_scalar_prefetch=1,
-            grid=(steps,),
-            in_specs=[
-                pl.BlockSpec((lines, lanes), lambda i, m: (0, 0)),
-                pl.BlockSpec(landed.shape, lambda i, m: (0, 0)),
-            ],
-            out_specs=pl.BlockSpec((length // steps, width), lambda i, m: (i, 0)),
-            scratch_shapes=[pltpu.VMEM((CAP + GROUP * lanes + ALIGN, width), landed.dtype)],
-        ),
+        unpack_kernel,
+        in_specs=[
+            pl.BlockSpec(memory_space=pltpu.SMEM),
+            pl.BlockSpec(memory_space=pltpu.VMEM),
+            pl.BlockSpec(memory_space=pltpu.VMEM),
+        ],
+        out_specs=pl.BlockSpec(memory_space=pl.ANY),
         out_shape=jax.ShapeDtypeStruct((length, width), landed.dtype),
+        scratch_shapes=[
+            pltpu.VMEM((CAP + 2 * lanes, width), landed.dtype),
+            pltpu.VMEM((lanes, lines), jnp.int32),
+            pltpu.VMEM((length, width), landed.dtype),
+            pltpu.SemaphoreType.DMA((LOADS,)),
+        ],
         compiler_params=pltpu.CompilerParams(vmem_limit_bytes=VMEM_LIMIT),
         name="unpack",
     )(info, places, landed)
@@ -806,7 +870,6 @@
 
     if (docs, ctx_count) == (2, 4) and local_len % (LINES * 128) == 0 and stripes >= 2 and shards >= 2:
         places, info = count(depth[0], plane, 0)
-        info = info[:, 0]
         dealt = compact(info, places, tokens, plane)
         weight = jnp.transpose(qkv_weight, (1, 0, 2))
         landed = block(info, LINES, dealt, weight, out_weight, docs, shards, stripes, 1)

time: 186 us -> 151 us (0.81)
  Pallas kernels: 184 us -> 150 us
    pallas_call x1, Pallas kernels: 161 us -> 130 us  [block(): pl.pallas_call(functools.partial(block_kernel, docs, first_meta), in_spec...]
    pallas_call x1, Pallas kernels: 8.38 us -> 4.32 us  [unpack(): pl.pallas_call(unpack_kernel, in_specs=[pl.BlockSpec(memory_space=pltpu.S...]
where the time goes in v3:
time: 151 us; the launch traced here: 150 us
  Pallas kernels  150 us (99%)
    pallas_call x1, Pallas kernels, block(): pl.pallas_call(functools.partial(block_kernel, docs, first_meta), in_spec...  130 us
    pallas_call x1, Pallas kernels, count(): pl.pallas_call(count_kernel, in_specs=[pl.BlockSpec(memory_space=pltpu.VM...  7.66 us
    pallas_call x1, Pallas kernels, compact(): pl.pallas_call(compact_kernel, in_specs=[pl.BlockSpec(memory_space=pltpu....  7.11 us
    pallas_call x1, Pallas kernels, unpack(): pl.pallas_call(unpack_kernel, in_specs=[pl.BlockSpec(memory_space=pltpu.S...  4.32 us

profile of v3, /device:TPU:0, one launch (start us, length us, event | category | flops | bytes accessed | tf_op | source)
XLA Modules:
  0.0 149.7 jit_solution(12187743520786071711)
XLA Ops:
  0.0 7.7 %count.1 = (s32[32,128]{1,0:T(8,128)}, s32[48,128]{1,0:T(8,128)}) custom-call(s32[32,128]{1,0:T(8,128)} %bitcast.7), custom_call_target="tpu_custom_call" | custom-call | tf_op jit(solution)/shard_map/count/pallas_call | solution.py:728
  7.7 7.1 %compact.1.deal_ref = bf16[8,128,640]{2,1,0:T(8,128)(2,1)} custom-call(s32[48,128]{1,0:T(8,128)} %get-tuple-element.7.info_ref.meta_ref, s32[32,128]{1,0:T(8,128)} %get-tuple-element.8.place_ref, bf16[4096,640]{1,0:T(8,128)(2,1)} %bitcast.5), custom_call_target="tpu_custom_call" | custom-call | tf_op jit(solution)/shard_map/compact/pallas_call | solution.py:793
  14.8 130.5 %block.1 = bf16[8,128,640]{2,1,0:T(8,128)(2,1)} custom-call(s32[48,128]{1,0:T(8,128)} %get-tuple-element.7.info_ref.meta_ref, bf16[8,128,640]{2,1,0:T(8,128)(2,1)} %compact.1.deal_ref, bf16[3,2560,640]{2,1,0:T(8,128)(2,1)} %bitcast.8, bf16[640,2560]{1,0:T(8,128)(2,1)} %wo_hbm.1), custom_call_target="tpu_custom_call" | custom-call | flops 10000000000 | bytes 100000000 | tf_op jit(solution)/shard_map/block/pallas_call | solution.py:619
  145.2 4.3 %unpack.1 = bf16[4096,640]{1,0:T(8,128)(2,1)} custom-call(s32[48,128]{1,0:T(8,128)} %get-tuple-element.7.info_ref.meta_ref, s32[32,128]{1,0:T(8,128)} %get-tuple-element.8.place_ref, bf16[1024,640]{1,0:T(8,128)(2,1)} %bitcast.6), custom_call_target="tpu_custom_call" | custom-call | tf_op jit(solution)/shard_map/unpack/pallas_call | solution.py:840

commit v4 on v3

--- a/solution.py
+++ b/solution.py
@@ -171,84 +171,132 @@
 
 
 ORDER = (
-    ("first", 0),
-    ("first", 1),
-    ("hop", 0, 1),
-    ("hop", 0, 2),
-    ("hop", 0, 3),
+    ("dsend", 0),
+    ("dsend", 1),
+    ("dwait", 0),
+    ("dsel", 0, 0),
+    ("dsel", 3, 0),
+    ("first", 0, 0),
+    ("hop", 0, 0, 1),
+    ("dwait", 1),
+    ("dsel", 0, 1),
+    ("dsel", 1, 0),
+    ("first", 0, 1),
+    ("hop", 0, 0, 2),
+    ("hop", 0, 0, 3),
+    ("dsel", 2, 1),
+    ("hop", 0, 1, 1),
+    ("dsel", 1, 1),
+    ("first", 1, 1),
+    ("hop", 0, 1, 2),
+    ("hop", 0, 1, 3),
+    ("first", 2, 1),
+    ("dsel", 2, 0),
+    ("hop", 1, 1, 1),
     ("pkv", 0),
-    ("hop", 1, 1),
+    ("first", 3, 0),
     ("own", 0),
+    ("first", 1, 0),
+    ("near", 0, 0),
+    ("hop", 1, 1, 2),
+    ("first", 2, 0),
+    ("dsel", 3, 1),
+    ("hop", 1, 0, 1),
+    ("hop", 1, 1, 3),
+    ("near", 0, 1),
     ("pq", 0),
-    ("first", 2),
-    ("near", 0, 0),
-    ("hop", 1, 2),
-    ("near", 0, 1),
-    ("hop", 1, 3),
-    ("hop", 2, 1),
+    ("hop", 1, 0, 2),
+    ("hop", 1, 0, 3),
+    ("first", 3, 1),
     ("pkv", 1),
-    ("first", 3),
+    ("hop", 2, 0, 1),
     ("far", 0, 0),
+    ("hop", 2, 1, 1),
+    ("far", 0, 1),
     ("own", 1),
-    ("hop", 2, 2),
-    ("far", 0, 1),
     ("pq", 1),
-    ("near", 1, 0),
     ("all", 0),
     ("late", 0),
-    ("hop", 3, 1),
     ("out", 0),
+    ("hop", 2, 1, 2),
+    ("hop", 2, 0, 2),
+    ("hop", 3, 1, 1),
+    ("rfirst", 0, 1),
+    ("near", 1, 0),
     ("near", 1, 1),
-    ("rfirst", 0),
-    ("hop", 2, 3),
+    ("hop", 2, 1, 3),
+    ("hop", 3, 0, 1),
+    ("hop", 2, 0, 3),
     ("pkv", 2),
+    ("pq", 2),
+    ("rfirst", 0, 0),
     ("own", 2),
-    ("pq", 2),
     ("far", 1, 0),
+    ("round", 0, 1, 1),
     ("early", 2, 0),
+    ("far", 1, 1),
     ("early", 1, 0),
-    ("far", 1, 1),
+    ("hop", 3, 1, 2),
     ("all", 1),
-    ("hop", 3, 2),
+    ("late", 1),
+    ("hop", 3, 1, 3),
     ("near", 2, 0),
-    ("late", 1),
-    ("hop", 3, 3),
     ("out", 1),
-    ("rfirst", 1),
-    ("round", 0, 1),
+    ("rfirst", 1, 0),
+    ("hop", 3, 0, 2),
+    ("round", 0, 0, 1),
+    ("hop", 3, 0, 3),
     ("pkv", 3),
     ("near", 2, 1),
-    ("pq", 3),
+    ("early", 2, 1),
+    ("rfirst", 1, 1),
     ("own", 3),
     ("far", 2, 0),
-    ("early", 2, 1),
-    ("round", 0, 2),
     ("far", 2, 1),
-    ("early", 3, 0),
     ("all", 2),
     ("late", 2),
-    ("round", 1, 1),
+    ("round", 0, 1, 2),
     ("out", 2),
-    ("round", 1, 2),
-    ("rfirst", 2),
     ("near", 3, 0),
+    ("round", 0, 0, 2),
+    ("round", 1, 1, 1),
+    ("rfirst", 2, 0),
+    ("pq", 3),
+    ("rfirst", 2, 1),
+    ("round", 1, 0, 1),
+    ("early", 3, 0),
     ("near", 3, 1),
-    ("final", 0),
-    ("round", 2, 1),
     ("early", 3, 1),
+    ("round", 2, 0, 1),
+    ("round", 1, 0, 2),
+    ("round", 1, 1, 2),
     ("far", 3, 0),
+    ("early", 3, 2),
     ("far", 3, 1),
-    ("early", 3, 2),
-    ("round", 2, 2),
+    ("round", 2, 0, 2),
     ("all", 3),
-    ("final", 1),
+    ("round", 2, 1, 1),
+    ("final", 1, 0),
     ("late", 3),
     ("out", 3),
-    ("rfirst", 3),
-    ("round", 3, 1),
-    ("round", 3, 2),
-    ("final", 2),
-    ("final", 3),
+    ("rfirst", 3, 0),
+    ("final", 1, 1),
+    ("final", 0, 1),
+    ("rfirst", 3, 1),
+    ("final", 2, 0),
+    ("final", 0, 0),
+    ("round", 3, 0, 1),
+    ("round", 3, 0, 2),
+    ("round", 3, 1, 1),
+    ("round", 2, 1, 2),
+    ("final", 3, 0),
+    ("bsend", 0),
+    ("round", 3, 1, 2),
+    ("final", 2, 1),
+    ("final", 3, 1),
+    ("bsend", 1),
+    ("bwait", 0),
+    ("bwait", 1),
 )
 
 
@@ -313,90 +361,120 @@
     def rows_of(s):
         return pl.ds(s * size, size)
 
-    def deal_copy(flip):
+    half = size // 2
+
+    def part_of_rows(s, part):
+        return pl.ds(s * size + part * half, half)
+
+    def part_rows(part):
+        return pl.ds(part * half, half)
+
+    def deal_copy(part, flip, origin):
         other, target = peer(flip)
-        return line_copy(deal_ref.at[other], received.at[me], d_send.at[flip], d_recv.at[flip], target)
-
-    def back_copy(flip):
+        at = part_rows(part)
+        return line_copy(
+            deal_ref.at[other, at], received.at[origin, at], d_send.at[part, flip], d_recv.at[part, flip], target
+        )
+
+    def back_copy(part, flip, origin):
         other, target = peer(flip)
-        return line_copy(returned.at[other], landed_ref.at[me], b_send.at[flip], b_recv.at[flip], target)
+        at = part_rows(part)
+        return line_copy(
+            returned.at[other, at], landed_ref.at[origin, at], b_send.at[part, flip], b_recv.at[part, flip], target
+        )
 
     far_first = (6, 7, 4, 5, 2, 3, 1)
 
-    def owned(b, s):
-        index = s * period + me * size + row
+    def owned(b, s, part):
+        index = s * period + me * size + part * half + row[:half]
         return (index >= meta_ref[first_meta + b, 0]) & (index < meta_ref[first_meta + b + 1, 0])
 
-    def deal():
+    def deal_send(part):
         for flip in far_first:
-            deal_copy(flip).start()
-        received[me] = deal_ref[me]
+            deal_copy(part, flip, me).start()
+        received[me, part_rows(part)] = deal_ref[me, part_rows(part)]
+
+    def deal_wait(part):
         for flip in far_first:
-            other, target = peer(flip)
-            line_copy(deal_ref.at[other], received.at[other], d_send.at[flip], d_recv.at[flip], target).wait_recv()
-        for s in range(stripes):
-            picked = jnp.zeros((size, width), jnp.float32)
-            for b in range(plane):
-                picked = jnp.where(owned(b, s), received[b].astype(jnp.float32), picked)
-            x_ref[rows_of(s)] = picked.astype(jnp.bfloat16)
-
-    def give_back():
+            deal_copy(part, flip, peer(flip)[0]).wait_recv()
+
+    def deal_pick(s, part):
+        picked = jnp.zeros((half, width), jnp.float32)
         for b in range(plane):
-            picked = jnp.zeros((size, width), jnp.float32)
+            picked = jnp.where(owned(b, s, part), received[b, part_rows(part)].astype(jnp.float32), picked)
+        picked = picked.astype(jnp.bfloat16)
+        x_ref[part_of_rows(s, part)] = picked
+        xg[z, part_of_rows(s, part)] = picked
+
+    def back_send(part):
+        for b in range(plane):
+            picked = jnp.zeros((half, width), jnp.float32)
             for s in range(stripes):
-                picked = jnp.where(owned(b, s), o_ref[rows_of(s)].astype(jnp.float32), picked)
-            returned[b] = picked.astype(jnp.bfloat16)
+                picked = jnp.where(owned(b, s, part), o_ref[part_of_rows(s, part)].astype(jnp.float32), picked)
+            returned[b, part_rows(part)] = picked.astype(jnp.bfloat16)
         for flip in far_first:
-            back_copy(flip).start()
-        landed_ref[me] = returned[me]
+            back_copy(part, flip, me).start()
+        landed_ref[me, part_rows(part)] = returned[me, part_rows(part)]
+
+    def back_wait(part):
         for flip in far_first:
-            other, target = peer(flip)
-            line_copy(returned.at[other], landed_ref.at[other], b_send.at[flip], b_recv.at[flip], target).wait_recv()
-        for flip in far_first:
-            deal_copy(flip).wait_send()
-            back_copy(flip).wait_send()
-
-    def feature_copy(s, way, hop):
+            back_copy(part, flip, peer(flip)[0]).wait_recv()
+
+    def deal_end():
+        for part in range(2):
+            for flip in far_first:
+                deal_copy(part, flip, me).wait_send()
+                back_copy(part, flip, me).wait_send()
+
+    def feature_copy(s, part, way, hop):
         origin = z + hop if way == 0 else z - hop
-        piece = xg.at[origin, rows_of(s)]
-        source = x_ref.at[rows_of(s)] if hop == 0 else piece
-        return line_copy(source, piece, a_send.at[way, s, hop], a_recv.at[way, s, hop], left if way == 0 else right)
+        at = part_of_rows(s, part)
+        piece = xg.at[origin, at]
+        source = x_ref.at[at] if hop == 0 else piece
+        return line_copy(
+            source, piece, a_send.at[way, s, part, hop], a_recv.at[way, s, part, hop], left if way == 0 else right
+        )
 
     def feature_sent(way, hop):
         return (z > 0) & (z + hop <= last) if way == 0 else (z < last) & (z - hop >= 0)
 
-    def feature_first(s):
+    def feature_first(s, part):
         for way in range(2):
 
             @pl.when(feature_sent(way, 0))
             def _():
-                feature_copy(s, way, 0).start()
-
-    def feature_hop(s, hop):
+                feature_copy(s, part, way, 0).start()
+
+    def feature_hop(s, part, hop):
         for way in range(2):
 
             @pl.when((z + hop <= last) if way == 0 else (z - hop >= 0))
             def _():
                 origin = z + hop if way == 0 else z - hop
-                piece = xg.at[origin, rows_of(s)]
+                piece = xg.at[origin, part_of_rows(s, part)]
                 line_copy(
-                    piece, piece, a_send.at[way, s, hop - 1], a_recv.at[way, s, hop - 1], left if way == 0 else right
+                    piece,
+                    piece,
+                    a_send.at[way, s, part, hop - 1],
+                    a_recv.at[way, s, part, hop - 1],
+                    left if way == 0 else right,
                 ).wait_recv()
 
             if hop < last:
 
                 @pl.when(feature_sent(way, hop))
                 def _():
-                    feature_copy(s, way, hop).start()
+                    feature_copy(s, part, way, hop).start()
 
     def feature_end():
         for s in range(stripes):
-            for way in range(2):
-                for hop in range(last):
-
-                    @pl.when(feature_sent(way, hop))
-                    def _():
-                        feature_copy(s, way, hop).wait_send()
+            for part in range(2):
+                for way in range(2):
+                    for hop in range(last):
+
+                        @pl.when(feature_sent(way, hop))
+                        def _():
+                            feature_copy(s, part, way, hop).wait_send()
 
     first = core == 0
     onward = jnp.where(first, block(0, 1, 0), block(1, 0, 0))
@@ -531,24 +609,30 @@
                 context[...], wo[:, j * width : (j + 1) * width], preferred_element_type=jnp.float32
             ).astype(jnp.bfloat16)
 
-    def sum_copy(s, way, d):
+    def sum_copy(s, part, way, d):
         land = from_right if way == 0 else from_left
+        at = part_rows(part)
         return line_copy(
-            terms.at[s, d], land.at[s, d], r_send.at[way, s, d], r_recv.at[way, s, d], left if way == 0 else right
+            terms.at[s, d, at],
+            land.at[s, d, at],
+            r_send.at[way, s, part, d],
+            r_recv.at[way, s, part, d],
+            left if way == 0 else right,
         )
 
     def sum_sent(way, d):
         return (z > d) if way == 0 else (z < d)
 
-    def sum_first(s):
+    def sum_first(s, part):
         for way in range(2):
             for k in range(last):
 
                 @pl.when(z == (last if way == 0 else 0))
                 def _():
-                    sum_copy(s, way, k if way == 0 else last - k).start()
-
-    def sum_round(s, r):
+                    sum_copy(s, part, way, k if way == 0 else last - k).start()
+
+    def sum_round(s, part, r):
+        at = part_rows(part)
         for way in range(2):
             land = from_right if way == 0 else from_left
             k = r - last + z if way == 0 else r - z
@@ -556,35 +640,40 @@
 
             @pl.when((k >= 0) & ((z < last) if way == 0 else (z > 0)))
             def _():
-                sum_copy(s, way, d).wait_recv()
-                terms[s, d] = (terms[s, d].astype(jnp.float32) + land[s, d].astype(jnp.float32)).astype(jnp.bfloat16)
-                sum_copy(s, way, d).start()
-
-    def sum_final(s):
-        final[...] = terms[s, z].astype(jnp.float32)
+                sum_copy(s, part, way, d).wait_recv()
+                sums = terms[s, d, at].astype(jnp.float32) + land[s, d, at].astype(jnp.float32)
+                terms[s, d, at] = sums.astype(jnp.bfloat16)
+                sum_copy(s, part, way, d).start()
+
+    def sum_final(s, part):
+        at = part_rows(part)
+        final[...] = terms[s, z, at].astype(jnp.float32)
         for way in range(2):
             land = from_right if way == 0 else from_left
 
             @pl.when((z < last) if way == 0 else (z > 0))
             def _():
-                sum_copy(s, way, z).wait_recv()
-                final[...] += land[s, z].astype(jnp.float32)
-
-        o_ref[rows_of(s)] = final[...].astype(jnp.bfloat16)
+                sum_copy(s, part, way, z).wait_recv()
+                final[...] += land[s, z, at].astype(jnp.float32)
+
+        o_ref[part_of_rows(s, part)] = final[...].astype(jnp.bfloat16)
 
     def sum_end():
         for s in range(stripes):
-            for way in range(2):
-                for d in range(shards):
-
-                    @pl.when(sum_sent(way, d))
-                    def _():
-                        sum_copy(s, way, d).wait_send()
-
-    deal()
-    for s in range(stripes):
-        xg[z, rows_of(s)] = x_ref[rows_of(s)]
+            for part in range(2):
+                for way in range(2):
+                    for d in range(shards):
+
+                        @pl.when(sum_sent(way, d))
+                        def _():
+                            sum_copy(s, part, way, d).wait_send()
+
     steps = {
+        "dsend": deal_send,
+        "dwait": deal_wait,
+        "dsel": deal_pick,
+        "bsend": back_send,
+        "bwait": back_wait,
         "first": feature_first,
         "hop": feature_hop,
         "pkv": project_kv,
@@ -602,7 +691,7 @@
     }
     for name, *at in ORDER:
         steps[name](*at)
-    give_back()
+    deal_end()
     feature_end()
     for copy in sent:
         copy.wait_send()
@@ -643,18 +732,18 @@
             pltpu.VMEM((stripes, shards, size, width), sixteen),
             pltpu.VMEM((stripes, shards, size, width), sixteen),
             pltpu.VMEM((stripes, shards, size, width), sixteen),
-            pltpu.VMEM((size, width), jnp.float32),
+            pltpu.VMEM((size // 2, width), jnp.float32),
             dma((4,)),
-            dma((2, stripes, shards)),
-            dma((2, stripes, shards)),
+            dma((2, stripes, 2, shards)),
+            dma((2, stripes, 2, shards)),
             dma((stripes, 2, 7)),
             dma((stripes, 2, 7)),
-            dma((2, stripes, shards)),
-            dma((2, stripes, shards)),
-            dma((plane,)),
-            dma((plane,)),
-            dma((plane,)),
-            dma((plane,)),
+            dma((2, stripes, 2, shards)),
+            dma((2, stripes, 2, shards)),
+            dma((2, plane)),
+            dma((2, plane)),
+            dma((2, plane)),
+            dma((2, plane)),
         ],
         compiler_params=pltpu.CompilerParams(
             collective_id=call, has_side_effects=True, vmem_limit_bytes=VMEM_LIMIT

time: 151 us -> 144 us (0.954)
  Pallas kernels: 150 us -> 143 us
    pallas_call x1, Pallas kernels: 130 us -> 124 us  [block(): pl.pallas_call(functools.partial(block_kernel, docs, first_meta), in_spec...]
where the time goes in v4:
time: 144 us; the launch traced here: 143 us
  Pallas kernels  143 us (99%)
    pallas_call x1, Pallas kernels, block(): pl.pallas_call(functools.partial(block_kernel, docs, first_meta), in_spec...  124 us
    pallas_call x1, Pallas kernels, count(): pl.pallas_call(count_kernel, in_specs=[pl.BlockSpec(memory_space=pltpu.VM...  7.66 us
    pallas_call x1, Pallas kernels, compact(): pl.pallas_call(compact_kernel, in_specs=[pl.BlockSpec(memory_space=pltpu....  7.11 us
    pallas_call x1, Pallas kernels, unpack(): pl.pallas_call(unpack_kernel, in_specs=[pl.BlockSpec(memory_space=pltpu.S...  4.32 us

profile of v4, /device:TPU:0, one launch (start us, length us, event | category | flops | bytes accessed | tf_op | source)
XLA Modules:
  0.0 143.2 jit_solution(4285315041705710199)
XLA Ops:
  0.0 7.7 %count.1 = (s32[32,128]{1,0:T(8,128)}, s32[48,128]{1,0:T(8,128)}) custom-call(s32[32,128]{1,0:T(8,128)} %bitcast.7), custom_call_target="tpu_custom_call" | custom-call | tf_op jit(solution)/shard_map/count/pallas_call | solution.py:817
  7.7 7.1 %compact.1.deal_ref = bf16[8,128,640]{2,1,0:T(8,128)(2,1)} custom-call(s32[48,128]{1,0:T(8,128)} %get-tuple-element.7.info_ref.meta_ref, s32[32,128]{1,0:T(8,128)} %get-tuple-element.8.place_ref, bf16[4096,640]{1,0:T(8,128)(2,1)} %bitcast.5), custom_call_target="tpu_custom_call" | custom-call | tf_op jit(solution)/shard_map/compact/pallas_call | solution.py:882
  14.8 123.9 %block.1 = bf16[8,128,640]{2,1,0:T(8,128)(2,1)} custom-call(s32[48,128]{1,0:T(8,128)} %get-tuple-element.7.info_ref.meta_ref, bf16[8,128,640]{2,1,0:T(8,128)(2,1)} %compact.1.deal_ref, bf16[3,2560,640]{2,1,0:T(8,128)(2,1)} %bitcast.8, bf16[640,2560]{1,0:T(8,128)(2,1)} %wo_hbm.1), custom_call_target="tpu_custom_call" | custom-call | flops 10000000000 | bytes 100000000 | tf_op jit(solution)/shard_map/block/pallas_call | solution.py:708
  138.7 4.3 %unpack.1 = bf16[4096,640]{1,0:T(8,128)(2,1)} custom-call(s32[48,128]{1,0:T(8,128)} %get-tuple-element.7.info_ref.meta_ref, s32[32,128]{1,0:T(8,128)} %get-tuple-element.8.place_ref, bf16[1024,640]{1,0:T(8,128)(2,1)} %bitcast.6), custom_call_target="tpu_custom_call" | custom-call | tf_op jit(solution)/shard_map/unpack/pallas_call | solution.py:929
